TPU v7x, 128 devices: a whole 4x4x4 slice. The times are simulated.
128 devices in a mesh: row: 8 (over z_lo, x), col: 16 (over y, z_hi, core).
Axes of the slice: x: 4, y: 4, z: 4 (z_hi: 2, z_lo: 2; z = z_hi * 2 + z_lo), core: 2. Of those that a mesh axis runs over, the one named last changes fastest.
Arguments:
- beats: bfloat16 [262144, 128], P(('row', 'col')), may hold values from -6 to 6
- track_marks: int32 [262144], P(('row', 'col')), may hold values 0 or 1
- valid_beats: int32 [128], replicated, may hold values from 64 to 2048, as said below
- pairing: int32 [2, 128], replicated, may hold values from 0 to 127, as said below
Outputs:
- profile: float32 [262144], P(('row', 'col'))
Inputs may be any that keep to these rules, and one draw needn't show every extreme that they name: `valid_beats`: each segment has at least 64 valid beats; some segment is full in every draw. pairing[0] pairs the segments of each grid column among themselves and pairing[1] those of each grid row; each row of pairing is an involution without fixed points.
All inputs are finite; a program needn't handle non-finite values. No bound on the sum of `track_marks` on one device may be relied on, other than what follows from the above.
Results may differ from a plain program's by a relative error of at most 0.0003.
Values may be sent and summed in bfloat16 or wider, within the bound.
No kernel may reach another device: no remote copies, remote signals or barrier semaphores. Data moves between devices by JAX's collectives and lax.ppermute only.
A program may use at most 128 MiB of HBM per device.

v0:
```python
import jax
import jax.numpy as jnp
from jax import lax
from jax.sharding import PartitionSpec as P

WIDTH = 128
SPAN = 64


CEIL = 4.0


def side_by_side(arrays, axis, dim, along):
    columns = [a.reshape(*a.shape[:along], -1) for a in arrays]
    both = jnp.concatenate(columns, axis=along)
    filled, at, outs = (lax.all_gather(both, axis, axis=dim, tiled=True), 0, [])
    for a, column in zip(arrays, columns):
        share = filled[..., at : at + column.shape[along]]
        outs.append(share.reshape(*share.shape[:along], *a.shape[along:]))
        at += column.shape[along]
    return tuple(outs)


def from_behind(block, axis, distance):
    devices = range(lax.axis_size(axis))
    route = [(i - distance, i) for i in devices if i - distance in devices]
    return lax.ppermute(block, axis, route)


def window_sum(values, count):
    total = values[0:count]
    for shift in range(1, SPAN):
        total = total + values[shift : shift + count]
    return total


def diagonal_window(gram):
    layered = gram
    window = 1
    offset = 0
    result = None
    while window <= SPAN:
        if SPAN & window:
            result = layered
            offset = offset + window
        if window * 2 <= SPAN:
            layered = layered[:-window, :-window] + layered[window:, window:]
        window = window * 2
    return result


def masked_block(
    left_ext,
    left_norm,
    left_live,
    left_pos,
    right_ext,
    right_norm,
    right_live,
    right_pos,
    left_count,
    right_count,
):
    right_rows = lax.slice_in_dim(right_ext, 0, right_count + SPAN - 1, axis=0)
    block_rows = min(512, left_count)
    block_total = left_count // block_rows

    def one_block(index):
        start = index * block_rows
        rows = lax.dynamic_slice_in_dim(left_ext, start, block_rows + SPAN - 1, 0)
        gram = lax.dot_general(
            rows, right_rows, (((1,), (1,)), ((), ())), preferred_element_type=jnp.float32
        )
        dots = diagonal_window(gram)
        norm_part = lax.dynamic_slice_in_dim(left_norm, start, block_rows, 0)
        live_part = lax.dynamic_slice_in_dim(left_live, start, block_rows, 0)
        pos_part = lax.dynamic_slice_in_dim(left_pos, start, block_rows, 0)
        dist = (norm_part[:, None] + right_norm[None, :] - 2.0 * dots) / (SPAN * WIDTH)
        allowed = (
            (live_part[:, None] > 0.5)
            & (right_live[None, :] > 0.5)
            & (jnp.abs(pos_part[:, None] - right_pos[None, :]) >= SPAN // 2)
        )
        masked = jnp.where(allowed, dist, CEIL)
        return (jnp.min(masked, axis=1), jnp.min(masked, axis=0))

    across, down = lax.map(one_block, jnp.arange(block_total, dtype=jnp.int32))
    return (across.reshape(left_count), jnp.min(down, axis=0))


def fetch_partner(own_ext, own_flags, target, axis_name):
    span_rows = own_ext.shape[0]

    def select(carry, pieces):
        ext_piece, flag_piece = pieces
        count = ext_piece.shape[0] // span_rows
        inside = (target >= 0) & (target < count)
        offset = jnp.clip(target, 0, count - 1) * span_rows
        taken_ext = lax.dynamic_slice_in_dim(ext_piece, offset, span_rows, 0)
        taken_flags = lax.dynamic_slice_in_dim(flag_piece, offset, span_rows, 0)
        return (jnp.where(inside, taken_ext, carry[0]), jnp.where(inside, taken_flags, carry[1]))

    empty = (jnp.zeros_like(own_ext), jnp.zeros_like(own_flags))
    if axis_name == "row":
        return select(
            empty,
            (
                lax.all_gather(own_ext, "row", axis=0, tiled=True),
                lax.all_gather(own_flags, "row", axis=0, tiled=True),
            ),
        )
    return select(empty, side_by_side((own_ext, own_flags), "col", 0, 1))


def meeting(own_ext, own_flags, own_norm, own_pos, partner, target, axis_name, seg_count):
    far_ext, far_flags = fetch_partner(own_ext, own_flags, target, axis_name)
    far_sq = jnp.sum(jnp.square(far_ext.astype(jnp.float32)), axis=1)
    far_norm = window_sum(far_sq, seg_count)
    offsets = jnp.arange(seg_count, dtype=jnp.int32)
    far_pos = partner * seg_count + offsets
    own_live = own_flags[:seg_count].astype(jnp.float32)
    far_live = far_flags[:seg_count].astype(jnp.float32)
    across, down = masked_block(
        own_ext,
        own_norm,
        own_live,
        own_pos,
        far_ext,
        far_norm,
        far_live,
        far_pos,
        seg_count,
        seg_count,
    )
    return across


def per_device(beats, track_marks, valid_beats, pairing):
    seg_count = beats.shape[0]
    col_count = lax.axis_size("col")
    total = valid_beats.shape[0]
    me = lax.axis_index("row") * col_count + lax.axis_index("col")
    marks = track_marks.astype(jnp.bfloat16)
    head_beats, head_marks = from_behind((beats[:SPAN], marks[:SPAN]), ("row", "col"), -1)
    own_ext = jnp.concatenate([beats, head_beats], 0)
    mark_ext = jnp.concatenate([marks, head_marks], 0).astype(jnp.float32)
    crossed = mark_ext[1 : 1 + seg_count]
    for shift in range(2, SPAN):
        crossed = crossed + mark_ext[shift : shift + seg_count]
    offsets = jnp.arange(seg_count, dtype=jnp.int32)
    valid_here = valid_beats[me]
    within = offsets + (SPAN - 1) < valid_here
    crossing = (valid_here == seg_count) & (me < total - 1)
    live = (within | crossing) & (crossed < 0.5)
    own_flags = jnp.concatenate([live.astype(jnp.bfloat16), jnp.zeros((SPAN,), jnp.bfloat16)], 0)
    own_sq = jnp.sum(jnp.square(own_ext.astype(jnp.float32)), axis=1)
    own_norm = window_sum(own_sq, seg_count)
    own_pos = me * seg_count + offsets
    first_partner = pairing[0, me]
    second_partner = pairing[1, me]
    first = meeting(
        own_ext,
        own_flags,
        own_norm,
        own_pos,
        first_partner,
        first_partner // col_count,
        "row",
        seg_count,
    )
    second = meeting(
        own_ext,
        own_flags,
        own_norm,
        own_pos,
        second_partner,
        second_partner % col_count,
        "col",
        seg_count,
    )
    return jnp.minimum(first, second)


def solution(mesh):
    placed = (P(("row", "col"), None), P(("row", "col")), P(), P())
    return jax.shard_map(
        per_device, mesh=mesh, in_specs=placed, out_specs=P(("row", "col")), check_vma=False
    )
```

profile of v0, /device:TPU:1, one launch (start us, length us, event | category | flops | bytes accessed | tf_op | source)
XLA Modules:
  0.0 245.9 jit_solution(6654244241761633937)
XLA Ops:
  7.3 3.3 %collective-permute-start.1 = (bf16[64,128]{1,0:T(8,128)(2,1)S(1)}, bf16[64,128]{1,0:T(8,128)(2,1)S(1)}, u32[]{:S(2)}, u32[]{:S(2)}) collective-permute-start(bf16[64,128]{1,0:T(8,128)(2,1)S(1)} %slice.927), channel_id=1, source_target_pairs={{1,0},{2,1},{3,2},{4,3},{5,4},{6,5},{7,6},{8,7},{9,8},{10,9},{11,1... | collective-permute-start | bytes 49160 | tf_op jit(solution)/shard_map/ppermute | solution.py:27
  11.6 3.9 %collective-permute-done.1 = bf16[64,128]{1,0:T(8,128)(2,1)S(1)} collective-permute-done((bf16[64,128]{1,0:T(8,128)(2,1)S(1)}, bf16[64,128]{1,0:T(8,128)(2,1)S(1)}, u32[]{:S(2)}, u32[]{:S(2)}) %collective-permute-start.1) | collective-permute-done | bytes 16416 | tf_op jit(solution)/shard_map/ppermute | solution.py:27
  17.2 1.9 collective-permute-start
  31.5 33.8 %all-reduce.1 = bf16[16896]{0:T(1024)(128)(2,1)S(1)} all-reduce(bf16[16896]{0:T(1024)(128)(2,1)S(1)} %dynamic-update-slice), channel_id=1, replica_groups=mesh['row'=8,'col'=16] {'row'}, use_global_device_ids=true, to_apply=%add.1 | all-reduce | flops 16896 | bytes 67584
  68.9 6.3 %all-gather.4.cloned.1.call-done = bf16[16896,128]{1,0:T(8,128)(2,1)} async-done(((bf16[2112,128]{1,0:T(8,128)(2,1)}), bf16[16896,128]{1,0:T(8,128)(2,1)}) %all-gather.4.cloned.1.call-update) | async-done | bytes 4325392 | tf_op jit(solution)/shard_map/all_gather | solution.py:108
  76.9 54.8 %while.22 = (s32[]{:T(128)}, f32[4,512]{1,0:T(4,128)S(1)}, s32[4]{0:T(128)S(1)}, f32[2048]{0:T(1024)S(1)}, f32[2048]{0:T(1024)S(1)}, /*index=5*/s32[2048]{0:T(10...) while((s32[]{:T(128)}, f32[4,512]{1,0:T(4,128)S(1)}, ...), condition=%wide.region_4.5_spmd.clone, body=%wide.region_2.4_spmd.clone.sunk | while | flops 329243456 | bytes 84997864 | solution.py:87
  79.5 1.8 slice_add_fusion.273
  81.3 1.8 slice_add_fusion.274
  87.4 3.2 %fusion.42 = f32[512]{0:T(512)S(1)} fusion(f32[544,2080]{1,0:T(8,128)S(1)} %slice_add_fusion.277, f32[2048]{0:T(1024)S(1)} %get-tuple-element.418, f32[512]{0:T(512)S(1)} %dynamic_slice.94, s32[2048]{0:T(1024)S(1)} %iota_add_fusion.5, s32[512]{0:T(512)S(1)} %dynamic_slice.95, pred[2048]{0:T(1024)(128)(4,1)S(1)} %broadcast_compare_fusion.4, ...), kind=kLoop, calls=%fused_computation.12.clone.1 | loop fusion | flops 12582400 | bytes 8413696 | tf_op jit(solution)/shard_map/while/body/eval_jaxpr/reduce_min | solution.py:85
  93.1 1.8 slice_add_fusion.273
  94.9 1.8 slice_add_fusion.274
  101.0 3.2 %fusion.42 = f32[512]{0:T(512)S(1)} fusion(f32[544,2080]{1,0:T(8,128)S(1)} %slice_add_fusion.277, f32[2048]{0:T(1024)S(1)} %get-tuple-element.418, f32[512]{0:T(512)S(1)} %dynamic_slice.94, s32[2048]{0:T(1024)S(1)} %iota_add_fusion.5, s32[512]{0:T(512)S(1)} %dynamic_slice.95, pred[2048]{0:T(1024)(128)(4,1)S(1)} %broadcast_compare_fusion.4, ...), kind=kLoop, calls=%fused_computation.12.clone.1 | loop fusion | flops 12582400 | bytes 8413696 | tf_op jit(solution)/shard_map/while/body/eval_jaxpr/reduce_min | solution.py:85
  106.8 1.8 slice_add_fusion.273
  114.7 3.2 %fusion.42 = f32[512]{0:T(512)S(1)} fusion(f32[544,2080]{1,0:T(8,128)S(1)} %slice_add_fusion.277, f32[2048]{0:T(1024)S(1)} %get-tuple-element.418, f32[512]{0:T(512)S(1)} %dynamic_slice.94, s32[2048]{0:T(1024)S(1)} %iota_add_fusion.5, s32[512]{0:T(512)S(1)} %dynamic_slice.95, pred[2048]{0:T(1024)(128)(4,1)S(1)} %broadcast_compare_fusion.4, ...), kind=kLoop, calls=%fused_computation.12.clone.1 | loop fusion | flops 12582400 | bytes 8413696 | tf_op jit(solution)/shard_map/while/body/eval_jaxpr/reduce_min | solution.py:85
  128.3 3.2 %fusion.42 = f32[512]{0:T(512)S(1)} fusion(f32[544,2080]{1,0:T(8,128)S(1)} %slice_add_fusion.277, f32[2048]{0:T(1024)S(1)} %get-tuple-element.418, f32[512]{0:T(512)S(1)} %dynamic_slice.94, s32[2048]{0:T(1024)S(1)} %iota_add_fusion.5, s32[512]{0:T(512)S(1)} %dynamic_slice.95, pred[2048]{0:T(1024)(128)(4,1)S(1)} %broadcast_compare_fusion.4, ...), kind=kLoop, calls=%fused_computation.12.clone.1 | loop fusion | flops 12582400 | bytes 8413696 | tf_op jit(solution)/shard_map/while/body/eval_jaxpr/reduce_min | solution.py:85
  131.6 22.5 %all-gather.6.cloned.1.call-done = bf16[16,2112,129]{1,2,0:T(8,128)(2,1)} async-done(((bf16[1,2112,129]{1,2,0:T(8,128)(2,1)}), bf16[16,2112,129]{1,2,0:T(8,128)(2,1)}) %all-gather.6.cloned.1.call-update) | async-done | bytes 8718352 | tf_op jit(solution)/shard_map/all_gather | solution.py:16
  154.1 20.0 %copy.15 = bf16[16,2112,129]{2,1,0:T(8,128)(2,1)} copy(bf16[16,2112,129]{1,2,0:T(8,128)(2,1)} %all-gather.6.cloned.1.call-done) | data formatting | bytes 17436672 | tf_op jit(solution)/shard_map/all_gather | solution.py:16
  174.1 5.4 %slice.1367 = bf16[33792,128]{1,0:T(8,128)(2,1)S(1)} slice(bf16[33792,129]{1,0:T(8,128)(2,1)} %bitcast.30), slice={[0:33792], [0:128]} | slice | bytes 17301504 | tf_op jit(solution)/shard_map/slice | solution.py:18
  179.6 3.1 %copy-done = bf16[16,2112,129]{2,1,0:T(8,128)(2,1)S(1)} copy-done((bf16[16,2112,129]{2,1,0:T(8,128)(2,1)S(1)}, bf16[16,2112,129]{2,1,0:T(8,128)(2,1)}, u32[]{:S(2)}) %copy-start) | copy-done | bytes 8718360
  184.1 54.3 %while.23 = (s32[]{:T(128)}, f32[4,512]{1,0:T(4,128)S(1)}, s32[4]{0:T(128)S(1)}, f32[2048]{0:T(1024)S(1)}, f32[2048]{0:T(1024)S(1)}, /*index=5*/s32[2048]{0:T(10...) while((s32[]{:T(128)}, f32[4,512]{1,0:T(4,128)S(1)}, ...), condition=%wide.region_8.9_spmd.clone, body=%wide.region_6.8_spmd.clone.sunk | while | flops 329243456 | bytes 84997864 | solution.py:87
  194.6 3.2 %fusion.46 = f32[512]{0:T(512)S(1)} fusion(f32[544,2080]{1,0:T(8,128)S(1)} %slice_add_fusion.282, f32[2048]{0:T(1024)S(1)} %get-tuple-element.466, f32[512]{0:T(512)S(1)} %dynamic_slice.99, s32[2048]{0:T(1024)S(1)} %iota_add_fusion.6, s32[512]{0:T(512)S(1)} %dynamic_slice.100, pred[2048]{0:T(1024)(128)(4,1)S(1)} %broadcast_compare_fusion.5, ...), kind=kLoop, calls=%fused_computation.31.clone.1 | loop fusion | flops 12582400 | bytes 8413696 | tf_op jit(solution)/shard_map/while/body/eval_jaxpr/reduce_min | solution.py:85
  208.1 3.2 %fusion.46 = f32[512]{0:T(512)S(1)} fusion(f32[544,2080]{1,0:T(8,128)S(1)} %slice_add_fusion.282, f32[2048]{0:T(1024)S(1)} %get-tuple-element.466, f32[512]{0:T(512)S(1)} %dynamic_slice.99, s32[2048]{0:T(1024)S(1)} %iota_add_fusion.6, s32[512]{0:T(512)S(1)} %dynamic_slice.100, pred[2048]{0:T(1024)(128)(4,1)S(1)} %broadcast_compare_fusion.5, ...), kind=kLoop, calls=%fused_computation.31.clone.1 | loop fusion | flops 12582400 | bytes 8413696 | tf_op jit(solution)/shard_map/while/body/eval_jaxpr/reduce_min | solution.py:85
  221.7 3.2 %fusion.46 = f32[512]{0:T(512)S(1)} fusion(f32[544,2080]{1,0:T(8,128)S(1)} %slice_add_fusion.282, f32[2048]{0:T(1024)S(1)} %get-tuple-element.466, f32[512]{0:T(512)S(1)} %dynamic_slice.99, s32[2048]{0:T(1024)S(1)} %iota_add_fusion.6, s32[512]{0:T(512)S(1)} %dynamic_slice.100, pred[2048]{0:T(1024)(128)(4,1)S(1)} %broadcast_compare_fusion.5, ...), kind=kLoop, calls=%fused_computation.31.clone.1 | loop fusion | flops 12582400 | bytes 8413696 | tf_op jit(solution)/shard_map/while/body/eval_jaxpr/reduce_min | solution.py:85
  235.2 3.2 %fusion.46 = f32[512]{0:T(512)S(1)} fusion(f32[544,2080]{1,0:T(8,128)S(1)} %slice_add_fusion.282, f32[2048]{0:T(1024)S(1)} %get-tuple-element.466, f32[512]{0:T(512)S(1)} %dynamic_slice.99, s32[2048]{0:T(1024)S(1)} %iota_add_fusion.6, s32[512]{0:T(512)S(1)} %dynamic_slice.100, pred[2048]{0:T(1024)(128)(4,1)S(1)} %broadcast_compare_fusion.5, ...), kind=kLoop, calls=%fused_computation.31.clone.1 | loop fusion | flops 12582400 | bytes 8413696 | tf_op jit(solution)/shard_map/while/body/eval_jaxpr/reduce_min | solution.py:85
  (141 shorter events, 84.1 us)
Async XLA Ops:
  6.5 68.7 %all-gather.4.cloned.1.call-start = ((), (), s32[]{:S(2)}) async-start(), calls=%async_computation | async-start | bytes 4866048 | tf_op jit(solution)/shard_map/all_gather | solution.py:108
  7.3 8.3 %collective-permute-start.1 = (bf16[64,128]{1,0:T(8,128)(2,1)S(1)}, bf16[64,128]{1,0:T(8,128)(2,1)S(1)}, u32[]{:S(2)}, u32[]{:S(2)}) collective-permute-start(bf16[64,128]{1,0:T(8,128)(2,1)S(1)} %slice.927), channel_id=1, source_target_pairs={{1,0},{2,1},{3,2},{4,3},{5,4},{6,5},{7,6},{8,7},{9,8},{10,9},{11,1... | collective-permute-start | bytes 49160 | tf_op jit(solution)/shard_map/ppermute | solution.py:27
  15.6 0.8 copy-start.1
  16.4 51.9 %copy-start.2 = (bf16[2112,128]{1,0:T(8,128)(2,1)S(1)}, bf16[2112,128]{1,0:T(8,128)(2,1)}, u32[]{:S(2)}) copy-start(bf16[2112,128]{1,0:T(8,128)(2,1)} %copy-done.1) | copy-start | bytes 1622020
  16.4 137.8 %all-gather.6.cloned.1.call-start = ((), (), s32[]{:S(2)}) async-start(), calls=%async_computation.1 | async-start | bytes 10061824 | tf_op jit(solution)/shard_map/all_gather | solution.py:16
  17.2 12.8 %collective-permute-start = (bf16[64]{0:T(256)(128)(2,1)S(1)}, bf16[64]{0:T(256)(128)(2,1)S(1)}, u32[]{:S(2)}, u32[]{:S(2)}) collective-permute-start(bf16[64]{0:T(256)(128)(2,1)S(1)} %slice.1173), channel_id=1, source_target_pairs={{1,0},{2,1},{3,2},{4,3},{5,4},{6,5},{7,6},{8,7},{9,8},{10,9},{11,1... | collective-permute-start | bytes 392 | tf_op jit(solution)/shard_map/ppermute | solution.py:27
  174.1 8.5 %copy-start = (bf16[16,2112,129]{2,1,0:T(8,128)(2,1)S(1)}, bf16[16,2112,129]{2,1,0:T(8,128)(2,1)}, u32[]{:S(2)}) copy-start(bf16[16,2112,129]{2,1,0:T(8,128)(2,1)} %copy.15) | copy-start | bytes 26155012
Sparse Core Ops, SparseCore 0:
  16.5 58.6 all-gather.3
  77.7 76.3 all-gather.5
where the time goes:
time: 247 us; the launch traced here: 246 us
  other arithmetic  95.5 us (39%)
  local copies, waits for them, and re-layouts  45.1 us (18%)
  blocking collectives  33.8 us (14%)
  waiting for transfers between devices  32.8 us (13%)
  between operations  20.5 us (8%)
  matrix products  6.57 us (3%)
  loops' own time  6.33 us (3%)
  starting transfers between devices  5.23 us (2%)
    add x40, other arithmetic, diagonal_window(): layered = layered[:-window, :-window] + layered[window:, window:]  63 us
    unnamed x1, blocking collectives  33.8 us
    reduce_min x8, other arithmetic, one_block(): return (jnp.min(masked, axis=1), jnp.min(masked, axis=0))  25.8 us
    all_gather x1, waiting for transfers between devices, side_by_side(): filled, at, outs = (lax.all_gather(both, axis, axis=dim, tiled=True), 0, [])  22.5 us
    all_gather x1, local copies, waits for them, and re-layouts, side_by_side(): filled, at, outs = (lax.all_gather(both, axis, axis=dim, tiled=True), 0, [])  20 us
    unnamed x12, local copies, waits for them, and re-layouts  8.71 us
    dot_general x8, matrix products, one_block(): lax.dot_general(rows, right_rows, (((1,), (1,)), ((), ())), preferred_ele...  6.57 us
    another operation x2, loops' own time, masked_block(): across, down = lax.map(one_block, jnp.arange(block_total, dtype=jnp.int32))  6.33 us
  transfers between devices with their start and end apart: 4, of which 3 were waited for; matrix products, arithmetic and copies ran while one was open for 26% of the time, Pallas kernels for 0%

commit v1 on v0

v1 whole, which is shorter than its diff:
```python
import functools

import jax
import jax.numpy as jnp
from jax import lax
from jax.experimental import pallas as pl
from jax.experimental.pallas import tpu as pltpu
from jax.sharding import PartitionSpec as P

WIDTH = 128
SPAN = 64
CEIL = 4.0
SEG = 2048
DEVS = 128
LANES = 128
SUBS = 8
STEP = SEG // SUBS
FOLD = 17
WRAP = FOLD * LANES
CHUNK = 16
SLOT1 = 24
SLOT2 = 40
DEAD = float(2**24)
F32 = jnp.float32
BF16 = jnp.bfloat16
VMEM = pltpu.VMEM


def scatter_kernel(beats_ref, marks_ref, out_ref, wide, flags):
    wide[0:SEG, :] = beats_ref[...].astype(F32)
    marks = marks_ref[...].astype(F32)
    flags[...] = marks
    pad = jnp.zeros((LANES - 2 * SUBS, LANES), F32)
    sub = lax.broadcasted_iota(jnp.int32, (SUBS, LANES), 0)
    turned = []
    for half in range(2):
        block = flags[pl.ds(half, SUBS, stride=2), :]
        extra = jnp.where(sub == 0, block, 0.0)
        turned.append(jnp.transpose(jnp.concatenate([block, extra, pad], 0)))
    flags2 = jnp.concatenate(turned, 0)
    out_ref[:, CHUNK:SLOT1, :] = jnp.zeros((DEVS, SUBS, LANES), BF16)
    wide[pl.ds(SEG, 2 * LANES), :] = flags2

    def one(k, _):
        first = wide[pl.ds(2 * k, SUBS, stride=STEP), :]
        second = wide[pl.ds(2 * k + 1, SUBS, stride=STEP), :]
        out_ref[k, 0:CHUNK, :] = jnp.concatenate([first, second], 0).astype(BF16)
        mark0 = wide[pl.ds(SEG + 2 * k, SUBS, stride=0), :]
        mark1 = wide[pl.ds(SEG + 2 * k + 1, SUBS, stride=0), :]
        beat0 = wide[pl.ds(2 * k, SUBS, stride=0), :]
        beat1 = wide[pl.ds(2 * k + 1, SUBS, stride=0), :]
        even = jnp.where(sub < 4, mark0, beat0)
        odd = jnp.where(sub < 4, mark1, beat1)
        rest = jnp.where((sub & 1) == 0, even, odd)
        out_ref[k, CHUNK:SLOT1, :] = rest.astype(BF16)
        return 0

    lax.fori_loop(0, DEVS, one, 0, unroll=4)


def route_kernel(pick_ref, got_ref, out_ref):
    sub = lax.broadcasted_iota(jnp.int32, (SUBS, LANES), 0)
    lane = lax.broadcasted_iota(jnp.int32, (SUBS, LANES), 1)
    marks = (sub < 4) & (lane < SUBS)
    to_first = ((sub < 4) & (sub < 2)) | (sub == 4) | (sub == 5)

    def one(d, _):
        first, second = pick_ref[0, d], pick_ref[1, d]
        after1, after2 = pick_ref[2, d], pick_ref[3, d]
        out_ref[d, 0:CHUNK, :] = got_ref[first, 0:CHUNK, :]
        out_ref[d, CHUNK : 2 * CHUNK, :] = got_ref[second, 0:CHUNK, :]
        mark1 = got_ref[first, CHUNK:SLOT1, :].astype(F32)
        mark2 = got_ref[second, CHUNK:SLOT1, :].astype(F32)
        next1 = got_ref[after1, CHUNK:SLOT1, :].astype(F32)
        next2 = got_ref[after2, CHUNK:SLOT1, :].astype(F32)
        own = jnp.where(to_first, mark1, mark2)
        behind = jnp.where(to_first, next1, next2)
        out_ref[d, 2 * CHUNK : SLOT2, :] = jnp.where(marks, own, behind).astype(BF16)
        return 0

    lax.fori_loop(0, DEVS, one, 0, unroll=4)


def join_kernel(info_ref, got_ref, own_ref, head_ref, out_ref, wide, right, left, prod, squares, extra, gates, bias):
    sub = lax.broadcasted_iota(jnp.int32, (SUBS, LANES), 0)
    lane = lax.broadcasted_iota(jnp.int32, (SUBS, LANES), 1)
    me = info_ref[0]

    wide[0:SPAN, :] = jnp.zeros((SPAN, LANES), F32)
    wide[pl.ds(SPAN, SEG), :] = own_ref[...].astype(F32)
    wide[pl.ds(SPAN + SEG, SPAN), :] = head_ref[0:SPAN, :].astype(F32)
    wide[pl.ds(2 * SPAN + SEG, SPAN), :] = jnp.zeros((SPAN, LANES), F32)
    for j in range(FOLD):
        here = wide[pl.ds(SPAN + j, LANES, stride=FOLD), :]
        back = wide[pl.ds(j, LANES, stride=FOLD), :]
        right[j * LANES : (j + 1) * LANES, 0:LANES] = (here * -2.0).astype(BF16)
        right[j * LANES : (j + 1) * LANES, LANES:] = (back * 2.0).astype(BF16)

    def widen(k, _):
        extra[pl.ds(pl.multiple_of(k * SUBS, SUBS), SUBS), :] = got_ref[k, 2 * CHUNK : SLOT2, :].astype(F32)
        return 0

    lax.fori_loop(0, DEVS, widen, 0, unroll=4)
    left[0 : SPAN * SUBS, LANES:] = jnp.zeros((SPAN * SUBS, LANES), BF16)

    row = lax.broadcasted_iota(jnp.int32, (STEP, LANES), 0)
    column = lax.broadcasted_iota(jnp.int32, (STEP, LANES), 1)

    def band(offset):
        gap = 2 * column + offset - row
        return jnp.where((gap >= 1) & (gap < SPAN), 1.0, 0.0).astype(BF16)

    bands = jnp.concatenate([band(0), band(1), band(STEP), band(STEP + 1)], 1)
    place = STEP * column + row
    base = FOLD * lane - STEP * sub

    bias[SEG:, :] = jnp.full((SUBS, LANES), 3.0e38, F32)
    best = [jnp.full((SUBS, LANES), 3.0e38, F32) for _ in range(FOLD)]
    for part in range(2):
        partner, valid, crossing = info_ref[1 + part], info_ref[3 + part], info_ref[5 + part]

        even = extra[pl.ds(2 * part, DEVS, stride=SUBS), :]
        odd = extra[pl.ds(2 * part + 1, DEVS, stride=SUBS), :]
        marks = jnp.concatenate(
            [even, odd, pltpu.roll(even, LANES - 1, 1), pltpu.roll(odd, LANES - 1, 1)], 0
        ).astype(BF16)
        crossed = jnp.dot(bands, marks, preferred_element_type=F32)
        live = ((place + (SPAN - 1) < valid) | (crossing > 0)) & (crossed < 0.5)
        gates[0:STEP, :] = jnp.where(live, 0.0, DEAD)

        def fill(k, _, part=part):
            rows = got_ref[k, part * CHUNK : (part + 1) * CHUNK, :]
            at = pl.multiple_of(k * CHUNK, CHUNK)
            left[pl.ds(at, CHUNK), 0:LANES] = rows
            left[pl.ds(at + SPAN * SUBS, CHUNK), LANES:] = rows
            x = rows.astype(F32)
            squares[pl.ds(at, CHUNK), :] = x * x
            return 0

        lax.fori_loop(0, DEVS, fill, 0, unroll=4)

        def follow(k, _, part=part):
            x = got_ref[k, part * CHUNK : (part + 1) * CHUNK, :].astype(F32)
            halves = []
            for half in range(2):
                behind = extra[pl.ds(k * SUBS + 4 + 2 * part + half, SUBS, stride=0), :]
                moved = pltpu.roll(x[half * SUBS : (half + 1) * SUBS], SUBS - 1, 0)
                halves.append(jnp.where(sub == SUBS - 1, behind, moved))
            y = jnp.concatenate(halves, 0)
            at = pl.multiple_of(SEG + k * CHUNK, CHUNK)
            left[pl.ds(at, CHUNK), 0:LANES] = y.astype(BF16)
            squares[pl.ds(at, CHUNK), :] = y * y
            return 0

        lax.fori_loop(0, SPAN // 2, follow, 0, unroll=4)

        def square(u):
            return squares[pl.ds(pl.multiple_of(u * SUBS, SUBS), SUBS), :]

        start = lax.fori_loop(
            0, SPAN, lambda u, t: t + square(u), jnp.zeros((SUBS, LANES), F32), unroll=8
        )

        def norm(i, total):
            gate = jnp.where(sub == lane, gates[pl.ds(i, SUBS, stride=0), :], 0.0)
            flat = jnp.sum(total + gate, axis=1, keepdims=True)
            bias[pl.ds(pl.multiple_of(i * SUBS, SUBS), SUBS), :] = jnp.broadcast_to(flat, (SUBS, LANES))
            return total + (square(i + SPAN) - square(i))

        lax.fori_loop(0, STEP, norm, start, unroll=8)

        shift = base + (me - partner) * SEG

        def block(b, carry, keep):
            at = pl.multiple_of(b * 256, 256)
            prod[...] = lax.dot_general(
                left[pl.ds(at, 256), :], right[...], (((1,), (1,)), ((), ())), preferred_element_type=F32
            )

            def eight(g, carry):
                for r in range(8):
                    total, low = carry
                    total = [pltpu.roll(total[-1], 1, 1)] + list(total[:-1])
                    rows = pl.ds(pl.multiple_of((g * 8 + r) * SUBS, SUBS), SUBS)
                    total = [total[j] + prod[rows, j * LANES : (j + 1) * LANES] for j in range(FOLD)]
                    low = list(low)
                    i = b * 32 + g * 8 + r - (SPAN - 1)
                    if keep == "all" or keep == "masked":
                        add = bias[pl.ds(pl.multiple_of(i * SUBS, SUBS), SUBS), :]
                        for j in range(FOLD):
                            value = total[j] + add
                            if keep == "masked":
                                gap = shift + (j - (SPAN - 1) - i)
                                value = jnp.where(jnp.abs(gap) < SPAN // 2, 3.0e38, value)
                            low[j] = jnp.minimum(low[j], value)
                    carry = (total, low)
                return carry

            return lax.fori_loop(0, 4, eight, carry)

        total = [jnp.zeros((SUBS, LANES), F32) for _ in range(FOLD)]

        def last(carry):
            total, low = carry
            add = bias[0:SUBS, :]
            low = list(low)
            for j in range(FOLD):
                gap = shift + (j - (SPAN - 1))
                value = jnp.where(jnp.abs(gap) < SPAN // 2, 3.0e38, total[j] + add)
                low[j] = jnp.minimum(low[j], value)
            return (total, low)

        carry = (total, best)
        carry = lax.fori_loop(0, 2, lambda b, c: block(b, c, "none"), carry)
        carry = last(carry)
        carry = block(2, carry, "masked")
        carry = lax.fori_loop(3, 9, lambda b, c: block(b, c, "all"), carry)
        carry = block(9, carry, "masked")
        best = carry[1]

    for j in range(FOLD):
        out_ref[j : j + 1, :] = jnp.min(best[j], axis=0, keepdims=True)


def window_sum(values, count):
    total = values[0:count]
    for shift in range(1, SPAN):
        total = total + values[shift : shift + count]
    return total


def per_device(beats, track_marks, valid_beats, pairing):
    me = lax.axis_index("row") * lax.axis_size("col") + lax.axis_index("col")
    tail = pltpu.CompilerParams(vmem_limit_bytes=48 * 2**20)

    heads = jnp.concatenate(
        [beats[:SPAN], jnp.broadcast_to(track_marks[None, :LANES].astype(BF16), (SUBS, LANES))], 0
    )
    head = lax.ppermute(heads, ("row", "col"), [(i + 1, i) for i in range(DEVS - 1)])

    sent = pl.pallas_call(
        scatter_kernel,
        out_shape=jax.ShapeDtypeStruct((DEVS, SLOT1, LANES), BF16),
        in_specs=[pl.BlockSpec(memory_space=VMEM)] * 2,
        out_specs=pl.BlockSpec(memory_space=VMEM),
        scratch_shapes=[VMEM((SEG + 2 * LANES + SUBS, LANES), F32), VMEM((CHUNK, LANES), F32)],
        compiler_params=tail,
    )(beats, track_marks.reshape(CHUNK, LANES))
    spread = lax.all_to_all(sent, ("row", "col"), 0, 0, tiled=True)

    after = jnp.minimum(pairing + 1, DEVS - 1)
    routed = pl.pallas_call(
        route_kernel,
        out_shape=jax.ShapeDtypeStruct((DEVS, SLOT2, LANES), BF16),
        in_specs=[pl.BlockSpec(memory_space=pltpu.SMEM), pl.BlockSpec(memory_space=VMEM)],
        out_specs=pl.BlockSpec(memory_space=VMEM),
        compiler_params=tail,
    )(jnp.concatenate([pairing, after], 0), spread)
    got = lax.all_to_all(routed, ("row", "col"), 0, 0, tiled=True)

    partners = pairing[:, me]
    valid = valid_beats[partners]
    crossing = ((valid == SEG) & (partners < DEVS - 1)).astype(jnp.int32)
    info = jnp.concatenate([me[None].astype(jnp.int32), partners, valid, crossing], 0)
    lowest = pl.pallas_call(
        join_kernel,
        out_shape=jax.ShapeDtypeStruct((FOLD, LANES), F32),
        in_specs=[pl.BlockSpec(memory_space=pltpu.SMEM)] + [pl.BlockSpec(memory_space=VMEM)] * 3,
        out_specs=pl.BlockSpec(memory_space=VMEM),
        scratch_shapes=[
            VMEM((SEG + 3 * SPAN, LANES), F32),
            VMEM((WRAP, 2 * LANES), BF16),
            VMEM((SEG + SPAN * SUBS, 2 * LANES), BF16),
            VMEM((256, WRAP), F32),
            VMEM((SEG + SPAN * SUBS, LANES), F32),
            VMEM((DEVS * SUBS + SUBS, LANES), F32),
            VMEM((STEP + SUBS, LANES), F32),
            VMEM((SEG + SUBS, LANES), F32),
        ],
        compiler_params=tail,
    )(info, got, beats, head)

    own_sq = jnp.concatenate(
        [
            jnp.sum(jnp.square(beats.astype(F32)), axis=1),
            jnp.sum(jnp.square(head[:SPAN].astype(F32)), axis=1),
        ],
        0,
    )
    norm = window_sum(own_sq, SEG)
    marks = jnp.concatenate([track_marks.astype(F32), head[SPAN, :SPAN].astype(F32)], 0)
    crossed = marks[1 : 1 + SEG]
    for shift in range(2, SPAN):
        crossed = crossed + marks[shift : shift + SEG]
    offsets = jnp.arange(SEG, dtype=jnp.int32)
    within = offsets + (SPAN - 1) < valid_beats[me]
    over = (valid_beats[me] == SEG) & (me < DEVS - 1)
    live = (within | over) & (crossed < 0.5)
    flat = lowest.T.reshape(WRAP)[SPAN - 1 : SPAN - 1 + SEG]
    dist = (norm + flat) * (1.0 / (SPAN * WIDTH))
    return jnp.where(live, jnp.minimum(dist, CEIL), CEIL)


def solution(mesh):
    placed = (P(("row", "col"), None), P(("row", "col")), P(), P())
    return jax.shard_map(
        per_device, mesh=mesh, in_specs=placed, out_specs=P(("row", "col")), check_vma=False
    )
```

time: 247 us -> 89.6 us (0.36)
  other arithmetic: 95.5 us -> 2.4 us
  local copies, waits for them, and re-layouts: 45.1 us -> 3.3 us
  blocking collectives: 33.8 us -> 0 us
  Pallas kernels: 0 us -> 31.4 us
  between operations: 20.5 us -> 0.74 us
  starting transfers between devices: 5.23 us -> 19.3 us
  matrix products: 6.57 us -> 0 us
  loops' own time: 6.33 us -> 0 us
    add x52 -> x0, other arithmetic: 63.7 us -> none  [the longest x40 63 us: diagonal_window(): layered = layered[:-window, :-window] + layered[window:, window:]]
    unnamed x1 -> x0, blocking collectives: 33.8 us -> none
    pallas_call x0 -> x3, Pallas kernels: none -> 31.4 us  [the longest x1 26.7 us: per_device(): pl.pallas_call(join_kernel, out_shape=jax.ShapeDtypeStruct((FOLD, LANES),...]
    all_gather x2 -> x0, waiting for transfers between devices: 28.8 us -> none  [the longest x1 22.5 us: side_by_side(): filled, at, outs = (lax.all_gather(both, axis, axis=dim, tiled=True), 0, [])]
    reduce_min x8 -> x0, other arithmetic: 25.8 us -> none  [one_block(): return (jnp.min(masked, axis=1), jnp.min(masked, axis=0))]
    all_to_all x0 -> x2, waiting for transfers between devices: none -> 23.5 us  [the longest x1 16.1 us: per_device(): spread = lax.all_to_all(sent, ('row', 'col'), 0, 0, tiled=True)]
    all_gather x1 -> x0, local copies, waits for them, and re-layouts: 20 us -> none  [side_by_side(): filled, at, outs = (lax.all_gather(both, axis, axis=dim, tiled=True), 0, [])]
    all_to_all x0 -> x2, starting transfers between devices: none -> 16.4 us  [the longest x1 11.5 us: per_device(): spread = lax.all_to_all(sent, ('row', 'col'), 0, 0, tiled=True)]
  transfers between devices with their start and end apart: 4 -> 3, of which waited for: 3 -> 3; matrix products, arithmetic and copies ran while one was open for 26% -> 2% of each run, Pallas kernels for 0% -> 0%
where the time goes in v1:
time: 89.6 us; the launch traced here: 89.2 us
  waiting for transfers between devices  32.1 us (36%)
  Pallas kernels  31.4 us (35%)
  starting transfers between devices  19.3 us (22%)
  local copies, waits for them, and re-layouts  3.3 us (4%)
  other arithmetic  2.4 us (3%)
    pallas_call x1, Pallas kernels, per_device(): pl.pallas_call(join_kernel, out_shape=jax.ShapeDtypeStruct((FOLD, LANES),...  26.7 us
    all_to_all x1, waiting for transfers between devices, per_device(): spread = lax.all_to_all(sent, ('row', 'col'), 0, 0, tiled=True)  16.1 us
    all_to_all x1, starting transfers between devices, per_device(): spread = lax.all_to_all(sent, ('row', 'col'), 0, 0, tiled=True)  11.5 us
    ppermute x1, waiting for transfers between devices, per_device(): lax.ppermute(heads, ('row', 'col'), [(i + 1, i) for i in range(DEVS - 1)])  8.58 us
    all_to_all x1, waiting for transfers between devices, per_device(): got = lax.all_to_all(routed, ('row', 'col'), 0, 0, tiled=True)  7.43 us
    all_to_all x1, starting transfers between devices, per_device(): got = lax.all_to_all(routed, ('row', 'col'), 0, 0, tiled=True)  4.89 us
    ppermute x1, starting transfers between devices, per_device(): lax.ppermute(heads, ('row', 'col'), [(i + 1, i) for i in range(DEVS - 1)])  2.98 us
    pallas_call x1, Pallas kernels, per_device(): pl.pallas_call(route_kernel, out_shape=jax.ShapeDtypeStruct((DEVS, SLOT2,...  2.64 us
  transfers between devices with their start and end apart: 3, of which 3 were waited for; matrix products, arithmetic and copies ran while one was open for 2% of the time, Pallas kernels for 0%

profile of v1, /device:TPU:1, one launch (start us, length us, event | category | flops | bytes accessed | tf_op | source)
XLA Modules:
  0.0 89.2 jit_solution(2701795961663170942)
XLA Ops:
  0.0 1.0 %copy-done = bf16[2048,128]{1,0:T(8,128)(2,1)S(1)} copy-done((bf16[2048,128]{1,0:T(8,128)(2,1)S(1)}, bf16[2048,128]{1,0:T(8,128)(2,1)}, u32[]{:S(2)}) %copy-start) | copy-done | bytes 524312
  1.0 0.7 copy-done.2
  1.7 2.0 %shard_map.46 = bf16[128,24,128]{2,1,0:T(8,128)(2,1)} custom-call(bf16[2048,128]{1,0:T(8,128)(2,1)S(1)} %copy-done, s32[16,128]{1,0:T(8,128)S(1)} %bitcast.10), custom_call_target="tpu_custom_call" | custom-call | tf_op jit(solution)/shard_map/pallas_call | solution.py:241
  3.7 11.5 %all-to-all-start = ((bf16[128,24,128]{2,1,0:T(8,128)(2,1)}), bf16[128,24,128]{2,1,0:T(8,128)(2,1)S(1)}, u32[]{:S(2)}, u32[]{:S(2)}) async-start(bf16[128,24,128]{2,1,0:T(8,128)(2,1)} %shard_map.46), calls=%async_computation | async-start | bytes 1572864 | tf_op jit(solution)/shard_map/all_to_all | solution.py:249
  15.2 0.0 copy-done.5
  15.2 16.1 %all-to-all-done.got_ref = bf16[128,24,128]{2,1,0:T(8,128)(2,1)S(1)} async-done(((bf16[128,24,128]{2,1,0:T(8,128)(2,1)}), bf16[128,24,128]{2,1,0:T(8,128)(2,1)S(1)}, u32[]{:S(2)}, u32[]{:S(2)}) %all-to-all-start) | async-done | bytes 786464 | tf_op jit(solution)/shard_map/all_to_all | solution.py:249
  31.3 2.6 %shard_map.47 = bf16[128,40,128]{2,1,0:T(8,128)(2,1)} custom-call(s32[4,128]{1,0:T(4,128)S(1)} %pad_add_fusion.pick_ref, bf16[128,24,128]{2,1,0:T(8,128)(2,1)S(1)} %all-to-all-done.got_ref), custom_call_target="tpu_custom_call" | custom-call | tf_op jit(solution)/shard_map/pallas_call | solution.py:252
  34.0 4.9 %all-to-all-start.1 = ((bf16[128,40,128]{2,1,0:T(8,128)(2,1)}), bf16[128,40,128]{2,1,0:T(8,128)(2,1)S(1)}, u32[]{:S(2)}, u32[]{:S(2)}) async-start(bf16[128,40,128]{2,1,0:T(8,128)(2,1)} %shard_map.47), calls=%async_computation.1 | async-start | bytes 2621440 | tf_op jit(solution)/shard_map/all_to_all | solution.py:259
  38.9 0.0 copy-done.3
  38.9 0.0 slice-done
  38.9 3.0 %collective-permute-start = (bf16[72,128]{1,0:T(8,128)(2,1)S(1)}, bf16[72,128]{1,0:T(8,128)(2,1)S(1)}, u32[]{:S(2)}, u32[]{:S(2)}) collective-permute-start(bf16[72,128]{1,0:T(8,128)(2,1)S(1)} %pad_maximum_fusion), channel_id=1, source_target_pairs={{1,0},{2,1},{3,2},{4,3},{5,4},{6,5},{7,6},{8,7},{9,8},{10,9},{11,1... | collective-permute-start | bytes 55304 | tf_op jit(solution)/shard_map/ppermute | solution.py:239
  41.9 0.2 fusion.256
  42.1 0.0 copy-done.4
  42.1 0.6 gather_fusion
  42.8 0.3 multiply_reduce_fusion
  43.1 0.1 pad_add_fusion.1.info_ref
  43.2 0.6 dynamic_slice.7
  44.4 8.6 %collective-permute-done.head_ref = bf16[72,128]{1,0:T(8,128)(2,1)S(1)} collective-permute-done((bf16[72,128]{1,0:T(8,128)(2,1)S(1)}, bf16[72,128]{1,0:T(8,128)(2,1)S(1)}, u32[]{:S(2)}, u32[]{:S(2)}) %collective-permute-start) | collective-permute-done | bytes 18464 | tf_op jit(solution)/shard_map/ppermute | solution.py:239
  53.0 0.1 multiply_reduce_fusion.1
  53.1 7.4 %all-to-all-done.1.got_ref = bf16[128,40,128]{2,1,0:T(8,128)(2,1)S(1)} async-done(((bf16[128,40,128]{2,1,0:T(8,128)(2,1)}), bf16[128,40,128]{2,1,0:T(8,128)(2,1)S(1)}, u32[]{:S(2)}, u32[]{:S(2)}) %all-to-all-start.1) | async-done | bytes 1310752 | tf_op jit(solution)/shard_map/all_to_all | solution.py:259
  60.5 26.7 %shard_map.48 = f32[17,128]{1,0:T(8,128)S(1)} custom-call(s32[7]{0:T(128)S(1)} %pad_add_fusion.1.info_ref, bf16[128,40,128]{2,1,0:T(8,128)(2,1)S(1)} %all-to-all-done.1.got_ref, bf16[2048,128]{1,0:T(8,128)(2,1)S(1)} %copy-done.1, bf16[72,128]{1,0:T(8,128)(2,1)S(1)} %collective-permute-done.head_ref), custom_call_target="tpu_custom_call" | custom-call | tf_op jit(solution)/shard_map/pallas_call | solution.py:265
  87.3 0.1 copy.5
  87.4 0.2 reshape.11
  87.6 1.6 %fusion.6 = f32[2048]{0:T(1024)} fusion(f32[2048]{0:T(1024)S(1)} %multiply_reduce_fusion, f32[64]{0:T(128)S(1)} %multiply_reduce_fusion.1, f32[2176]{0:T(1024)S(1)} %reshape.11, f32[64]{0:T(128)S(1)} %fusion.257, f32[2048]{0:T(1024)S(1)} %convert_element_type.20, s32[]{:T(128)} %bitcast, pred[]{:T(512)S(6)} %and.11), kind=kLoop, calls=%fused_computation.258 | loop fusion | flops 532480 | bytes 33285 | tf_op jit(solution)/shard_map/jit(_where)/select_n | solution.py:301
  (17 shorter events, 0.1 us)
Async XLA Ops:
  0.0 1.0 %copy-start = (bf16[2048,128]{1,0:T(8,128)(2,1)S(1)}, bf16[2048,128]{1,0:T(8,128)(2,1)}, u32[]{:S(2)}) copy-start(bf16[2048,128]{1,0:T(8,128)(2,1)} %own_ref.1) | copy-start | bytes 1572868
  1.0 0.7 copy-start.2
  1.7 13.5 %copy-start.5 = (s32[2,128]{1,0:T(2,128)S(1)}, s32[2,128]{1,0:T(2,128)}, u32[]{:S(2)}) copy-start(s32[2,128]{1,0:T(2,128)} %param.7) | copy-start | bytes 3076
  3.7 27.6 %all-to-all-start = ((bf16[128,24,128]{2,1,0:T(8,128)(2,1)}), bf16[128,24,128]{2,1,0:T(8,128)(2,1)S(1)}, u32[]{:S(2)}, u32[]{:S(2)}) async-start(bf16[128,24,128]{2,1,0:T(8,128)(2,1)} %shard_map.46), calls=%async_computation | async-start | bytes 1572864 | tf_op jit(solution)/shard_map/all_to_all | solution.py:249
  34.0 4.9 %copy-start.3 = (s32[2048]{0:T(1024)S(1)}, s32[2048]{0:T(1024)}, u32[]{:S(2)}) copy-start(s32[2048]{0:T(1024)} %param.5) | copy-start | bytes 24580
  34.0 4.9 %slice-start = ((bf16[2048,128]{1,0:T(8,128)(2,1)}), bf16[64,128]{1,0:T(8,128)(2,1)S(1)}, s32[]{:S(2)}) async-start(bf16[2048,128]{1,0:T(8,128)(2,1)} %own_ref.1), calls=%async_computation.2 | async-start | bytes 32768 | tf_op jit(solution)/shard_map/slice | solution.py:237
  34.0 8.2 %copy-start.4 = (s32[128]{0:T(128)S(1)}, s32[128]{0:T(128)}, u32[]{:S(2)}) copy-start(s32[128]{0:T(128)} %param.6) | copy-start | bytes 1540
  34.0 8.8 %copy-start.1 = (bf16[2048,128]{1,0:T(8,128)(2,1)S(1)}, bf16[2048,128]{1,0:T(8,128)(2,1)}, u32[]{:S(2)}) copy-start(bf16[2048,128]{1,0:T(8,128)(2,1)} %own_ref.1) | copy-start | bytes 1572868
  34.0 26.5 %all-to-all-start.1 = ((bf16[128,40,128]{2,1,0:T(8,128)(2,1)}), bf16[128,40,128]{2,1,0:T(8,128)(2,1)S(1)}, u32[]{:S(2)}, u32[]{:S(2)}) async-start(bf16[128,40,128]{2,1,0:T(8,128)(2,1)} %shard_map.47), calls=%async_computation.1 | async-start | bytes 2621440 | tf_op jit(solution)/shard_map/all_to_all | solution.py:259
  38.9 14.0 %collective-permute-start = (bf16[72,128]{1,0:T(8,128)(2,1)S(1)}, bf16[72,128]{1,0:T(8,128)(2,1)S(1)}, u32[]{:S(2)}, u32[]{:S(2)}) collective-permute-start(bf16[72,128]{1,0:T(8,128)(2,1)S(1)} %pad_maximum_fusion), channel_id=1, source_target_pairs={{1,0},{2,1},{3,2},{4,3},{5,4},{6,5},{7,6},{8,7},{9,8},{10,9},{11,1... | collective-permute-start | bytes 55304 | tf_op jit(solution)/shard_map/ppermute | solution.py:239

commit v2 on v1

v2 whole, which is shorter than its diff:
```python
import functools

import jax
import jax.numpy as jnp
from jax import lax
from jax.experimental import pallas as pl
from jax.experimental.pallas import tpu as pltpu
from jax.sharding import PartitionSpec as P

WIDTH = 128
SPAN = 64
CEIL = 4.0
SEG = 2048
DEVS = 128
LANES = 128
SUBS = 8
STEP = SEG // SUBS
FOLD = 17
WRAP = FOLD * LANES
CHUNK = 16
SLOT = 24
SLOT2 = 40
EARLY = True
BLOCK = 512
DEAD = float(2**24)
F32 = jnp.float32
BF16 = jnp.bfloat16
VMEM = pltpu.VMEM


def scatter_kernel(beats_ref, marks_ref, out_ref, wide, flags):
    wide[0:SEG, :] = beats_ref[...].astype(F32)
    marks = marks_ref[...].astype(F32)
    flags[...] = marks
    pad = jnp.zeros((LANES - 2 * SUBS, LANES), F32)
    sub = lax.broadcasted_iota(jnp.int32, (SUBS, LANES), 0)
    turned = []
    for half in range(2):
        block = flags[pl.ds(half, SUBS, stride=2), :]
        extra = jnp.where(sub == 0, block, 0.0)
        turned.append(jnp.transpose(jnp.concatenate([block, extra, pad], 0)))
    flags2 = jnp.concatenate(turned, 0)
    out_ref[:, CHUNK:SLOT, :] = jnp.zeros((DEVS, SUBS, LANES), BF16)
    wide[pl.ds(SEG, 2 * LANES), :] = flags2

    def one(k, _):
        first = wide[pl.ds(2 * k, SUBS, stride=STEP), :]
        second = wide[pl.ds(2 * k + 1, SUBS, stride=STEP), :]
        out_ref[k, 0:CHUNK, :] = jnp.concatenate([first, second], 0).astype(BF16)
        mark0 = wide[pl.ds(SEG + 2 * k, SUBS, stride=0), :]
        mark1 = wide[pl.ds(SEG + 2 * k + 1, SUBS, stride=0), :]
        beat0 = wide[pl.ds(2 * k, SUBS, stride=0), :]
        beat1 = wide[pl.ds(2 * k + 1, SUBS, stride=0), :]
        even = jnp.where(sub < 4, mark0, beat0)
        odd = jnp.where(sub < 4, mark1, beat1)
        rest = jnp.where((sub & 1) == 0, even, odd)
        out_ref[k, CHUNK:SLOT, :] = rest.astype(BF16)
        return 0

    lax.fori_loop(0, DEVS, one, 0, unroll=4)


def route_kernel(pick_ref, got_ref, info_ref, right_ref, norm_ref, out_ref):
    sub = lax.broadcasted_iota(jnp.int32, (SUBS, LANES), 0)
    lane = lax.broadcasted_iota(jnp.int32, (SUBS, LANES), 1)
    marks = (sub < 4) & (lane < SUBS)
    to_first = (sub < 2) | (sub == 4) | (sub == 5)
    to_even = (sub & 1) == 0

    def one(d, _):
        first, second = pick_ref[0, d], pick_ref[1, d]
        after1, after2 = pick_ref[2, d], pick_ref[3, d]
        x = got_ref[first, 0:CHUNK, :].astype(F32)
        y = got_ref[second, 0:CHUNK, :].astype(F32)
        near, far = [], []
        for half in range(2):
            rows = slice(half * SUBS, (half + 1) * SUBS)
            near.append(jnp.where(to_even, x[rows], pltpu.roll(y[rows], 1, 0)))
            far.append(jnp.where(to_even, pltpu.roll(x[rows], SUBS - 1, 0), y[rows]))
        out_ref[d, 0:CHUNK, :] = jnp.concatenate(near, 0).astype(BF16)
        out_ref[d, CHUNK : 2 * CHUNK, :] = jnp.concatenate(far, 0).astype(BF16)
        mark1 = got_ref[first, CHUNK:SLOT, :].astype(F32)
        mark2 = got_ref[second, CHUNK:SLOT, :].astype(F32)
        next1 = got_ref[after1, CHUNK:SLOT, :].astype(F32)
        next2 = got_ref[after2, CHUNK:SLOT, :].astype(F32)
        own = jnp.where(to_first, mark1, mark2)
        behind = jnp.where(to_first, next1, next2)
        out_ref[d, 2 * CHUNK : SLOT2, :] = jnp.where(marks, own, behind).astype(BF16)
        return 0

    lax.fori_loop(0, DEVS, one, 0, unroll=4)


def own_kernel(own_ref, head_ref, out_ref, wide):
    wide[0:SPAN, :] = jnp.zeros((SPAN, LANES), F32)
    wide[pl.ds(SPAN, SEG), :] = own_ref[...].astype(F32)
    wide[pl.ds(SPAN + SEG, SPAN), :] = head_ref[0:SPAN, :].astype(F32)
    wide[pl.ds(2 * SPAN + SEG, SPAN), :] = jnp.zeros((SPAN, LANES), F32)
    for j in range(FOLD):
        here = wide[pl.ds(SPAN + j, LANES, stride=FOLD), :]
        back = wide[pl.ds(j, LANES, stride=FOLD), :]
        out_ref[j * LANES : (j + 1) * LANES, 0:LANES] = (here * -2.0).astype(BF16)
        out_ref[j * LANES : (j + 1) * LANES, LANES:] = (back * 2.0).astype(BF16)


def join_kernel(info_ref, got_ref, right, out_ref, tail, prod0, prod1, extra, gates, bias):
    sub = lax.broadcasted_iota(jnp.int32, (SUBS, LANES), 0)
    lane = lax.broadcasted_iota(jnp.int32, (SUBS, LANES), 1)
    me = info_ref[0]

    def fill(k, _):
        extra[pl.ds(pl.multiple_of(k * SUBS, SUBS), SUBS), :] = got_ref[k, 2 * CHUNK : SLOT2, :].astype(F32)
        return 0

    lax.fori_loop(0, DEVS, fill, 0, unroll=16)

    def follow(k, _):
        x = got_ref[k, 0:CHUNK, :].astype(F32)
        halves = []
        for half in range(2):
            behind1 = extra[pl.ds(k * SUBS + 4 + half, SUBS, stride=0), :]
            behind2 = extra[pl.ds(k * SUBS + 6 + half, SUBS, stride=0), :]
            moved = pltpu.roll(x[half * SUBS : (half + 1) * SUBS], SUBS - 2, 0)
            halves.append(jnp.where(sub == SUBS - 2, behind1, jnp.where(sub == SUBS - 1, behind2, moved)))
        y = jnp.concatenate(halves, 0)
        tail[pl.ds(pl.multiple_of(k * CHUNK, CHUNK), CHUNK), :] = y.astype(BF16)
        return 0

    lax.fori_loop(0, SPAN // 2, follow, 0, unroll=4)

    row = lax.broadcasted_iota(jnp.int32, (STEP, LANES), 0)
    column = lax.broadcasted_iota(jnp.int32, (STEP, LANES), 1)
    place = STEP * column + row

    def band(offset):
        gap = 2 * column + offset - row
        return jnp.where((gap >= 1) & (gap < SPAN), 1.0, 0.0).astype(BF16)

    bands = jnp.concatenate([band(0), band(1), band(STEP), band(STEP + 1)], 1)
    closed = []
    for part in range(2):
        even = extra[pl.ds(2 * part, DEVS, stride=SUBS), :]
        odd = extra[pl.ds(2 * part + 1, DEVS, stride=SUBS), :]
        marks = jnp.concatenate(
            [even, odd, pltpu.roll(even, LANES - 1, 1), pltpu.roll(odd, LANES - 1, 1)], 0
        ).astype(BF16)
        crossed = jnp.dot(bands, marks, preferred_element_type=F32)
        valid, crossing = info_ref[3 + part], info_ref[5 + part]
        live = ((place + (SPAN - 1) < valid) | (crossing > 0)) & (crossed < 0.5)
        closed.append(jnp.where(live, 0.0, DEAD))
    to_even = (column & 1) == 0
    gates[0:STEP, :] = jnp.where(to_even, closed[0], pltpu.roll(closed[1], 1, 1))
    gates[STEP : 2 * STEP, :] = jnp.where(to_even, pltpu.roll(closed[0], LANES - 1, 1), closed[1])

    def pair(u):
        if u < STEP:
            rows = got_ref[u // 2, 0:CHUNK, :]
        elif u < 2 * STEP:
            rows = got_ref[(u - STEP) // 2, CHUNK : 2 * CHUNK, :]
        else:
            at = (u - 2 * STEP) // 2 * CHUNK
            rows = tail[at : at + CHUNK, :]
        x = rows.astype(F32)
        return x * x

    def source(b):
        per = BLOCK // CHUNK
        if b < DEVS // per:
            return got_ref[b * per : (b + 1) * per, 0:CHUNK, :].reshape(BLOCK, LANES)
        b -= DEVS // per
        if b < DEVS // per:
            return got_ref[b * per : (b + 1) * per, CHUNK : 2 * CHUNK, :].reshape(BLOCK, LANES)
        b -= DEVS // per
        return tail[b * BLOCK : (b + 1) * BLOCK, :]

    base = FOLD * lane - 2 * STEP * (sub >> 1)
    partner = jnp.where((sub & 1) == 0, info_ref[1], info_ref[2])
    ahead = jnp.where(partner == me + 1, base, -(2**20))
    behind = jnp.where(partner == me - 1, base, 2**20)
    limit = SEG - SPAN // 2

    def dot(b, prod):
        past = b - SPAN * SUBS // BLOCK
        rows, depth = source(b), LANES
        if past >= 0:
            rows, depth = jnp.concatenate([rows, source(past)], 1), 2 * LANES
        prod[...] = lax.dot_general(
            rows, right[:, 0:depth], (((1,), (1,)), ((), ())), preferred_element_type=F32
        )

    steps = BLOCK // SUBS
    count = 2 * STEP
    blocks = (count + SPAN) // steps

    def norms(energy, first, last):
        for i in range(first, last):
            gate = jnp.where(sub == lane, gates[pl.ds(i, SUBS, stride=0), :], 0.0)
            flat = jnp.sum(energy + gate, axis=1, keepdims=True)
            bias[i * SUBS : (i + 1) * SUBS, :] = jnp.broadcast_to(flat, (SUBS, LANES))
            at = slice(i % 2 * SUBS, (i % 2 + 1) * SUBS)
            energy = energy + (pair(i + SPAN)[at] - pair(i)[at])
        return energy

    total = [jnp.zeros((SUBS, LANES), F32) for _ in range(FOLD)]
    low = [jnp.full((SUBS, LANES), 3.0e38, F32) for _ in range(FOLD)]
    prods = (prod0, prod1)
    dot(0, prods[0])
    energy = jnp.zeros((SUBS, LANES), F32)
    for u in range(0, SPAN, 2):
        both = pair(u)
        energy = energy + (both[0:SUBS] + both[SUBS:])
    made = 0
    for b in range(blocks):
        if b + 1 < blocks:
            dot(b + 1, prods[(b + 1) % 2])
        goal = min((b + 1) * steps - (SPAN - 1) + (steps if EARLY else 0), count)
        if goal > made:
            energy = norms(energy, made, goal)
            made = goal
        prod = prods[b % 2]
        for r in range(steps):
            i = b * steps + r - (SPAN - 1)
            if i >= count:
                break
            total = [pltpu.roll(total[-1], 1, 1)] + total[:-1]
            rows = slice(r * SUBS, (r + 1) * SUBS)
            total = [total[j] + prod[rows, j * LANES : (j + 1) * LANES] for j in range(FOLD)]
            if i < 0:
                continue
            add = bias[i * SUBS : (i + 1) * SUBS, :]
            for j in range(FOLD):
                value = total[j] + add
                offset = j - (SPAN - 1) - i
                if i < SPAN // 2 - 1:
                    value = jnp.where(ahead > limit - offset, 3.0e38, value)
                if i > count - SPAN // 2:
                    value = jnp.where(behind < -limit - offset, 3.0e38, value)
                low[j] = jnp.minimum(low[j], value)

    for j in range(FOLD):
        out_ref[j : j + 1, :] = jnp.min(low[j], axis=0, keepdims=True)


def window_sum(values, count):
    total = values[0:count]
    for shift in range(1, SPAN):
        total = total + values[shift : shift + count]
    return total


def per_device(beats, track_marks, valid_beats, pairing):
    me = lax.axis_index("row") * lax.axis_size("col") + lax.axis_index("col")

    def room(mib):
        return pltpu.CompilerParams(vmem_limit_bytes=mib * 2**20)

    vmem = pl.BlockSpec(memory_space=VMEM)
    smem = pl.BlockSpec(memory_space=pltpu.SMEM)

    sent = pl.pallas_call(
        scatter_kernel,
        out_shape=jax.ShapeDtypeStruct((DEVS, SLOT, LANES), BF16),
        in_specs=[vmem] * 2,
        out_specs=vmem,
        scratch_shapes=[VMEM((SEG + 2 * LANES + SUBS, LANES), F32), VMEM((CHUNK, LANES), F32)],
        compiler_params=room(56),
    )(beats, track_marks.reshape(CHUNK, LANES))
    sent, beats, track_marks = lax.optimization_barrier((sent, beats, track_marks))
    spread = lax.all_to_all(sent, ("row", "col"), 0, 0, tiled=True)

    heads = jnp.concatenate([beats[:SPAN], jnp.broadcast_to(track_marks[None, :LANES].astype(BF16), (SUBS, LANES))], 0)
    head = lax.ppermute(heads, ("row", "col"), [(i + 1, i) for i in range(DEVS - 1)])
    right = pl.pallas_call(
        own_kernel,
        out_shape=jax.ShapeDtypeStruct((WRAP, 2 * LANES), BF16),
        in_specs=[vmem] * 2,
        out_specs=vmem,
        scratch_shapes=[VMEM((SEG + 3 * SPAN, LANES), F32)],
        compiler_params=room(16),
    )(beats, head)
    own_sq = jnp.concatenate(
        [
            jnp.sum(jnp.square(beats.astype(F32)), axis=1),
            jnp.sum(jnp.square(head[:SPAN].astype(F32)), axis=1),
        ],
        0,
    )
    norm = window_sum(own_sq, SEG)
    marks = jnp.concatenate([track_marks.astype(F32), head[SPAN, :SPAN].astype(F32)], 0)
    crossed = marks[1 : 1 + SEG]
    for shift in range(2, SPAN):
        crossed = crossed + marks[shift : shift + SEG]
    offsets = jnp.arange(SEG, dtype=jnp.int32)
    within = offsets + (SPAN - 1) < valid_beats[me]
    over = (valid_beats[me] == SEG) & (me < DEVS - 1)
    live = (within | over) & (crossed < 0.5)
    norm = jnp.where(live, norm, DEAD)

    partners = pairing[:, me]
    valid = valid_beats[partners]
    crossing = ((valid == SEG) & (partners < DEVS - 1)).astype(jnp.int32)
    after = jnp.minimum(pairing + 1, DEVS - 1)
    info = jnp.concatenate([me[None].astype(jnp.int32), partners, valid, crossing], 0)
    picks = jnp.concatenate([pairing, after], 0)


    routed = pl.pallas_call(
        route_kernel,
        out_shape=jax.ShapeDtypeStruct((DEVS, SLOT2, LANES), BF16),
        in_specs=[smem, vmem, smem] + [pl.BlockSpec(memory_space=pl.ANY)] * 2,
        out_specs=vmem,
        compiler_params=room(16),
    )(picks, spread, info, right, norm)
    got = lax.all_to_all(routed, ("row", "col"), 0, 0, tiled=True)
    best = pl.pallas_call(
        join_kernel,
        out_shape=jax.ShapeDtypeStruct((FOLD, LANES), F32),
        in_specs=[smem] + [vmem] * 2,
        out_specs=vmem,
        scratch_shapes=[
            VMEM((SPAN * SUBS, LANES), BF16),
            VMEM((BLOCK, WRAP), F32),
            VMEM((BLOCK, WRAP), F32),
            VMEM((DEVS * SUBS + SUBS, LANES), F32),
            VMEM((2 * STEP + SUBS, LANES), F32),
            VMEM((2 * SEG, LANES), F32),
        ],
        compiler_params=room(36),
    )(info, got, right)
    flat = best.T.reshape(WRAP)[SPAN - 1 : SPAN - 1 + SEG]
    return jnp.minimum((norm + flat) * (1.0 / (SPAN * WIDTH)), CEIL)


def solution(mesh):
    placed = (P(("row", "col"), None), P(("row", "col")), P(), P())
    return jax.shard_map(
        per_device, mesh=mesh, in_specs=placed, out_specs=P(("row", "col")), check_vma=False
    )
```

time: 89.6 us -> 68.5 us (0.76)
  blocking collectives: 0 us -> 26.7 us
  waiting for transfers between devices: 32.1 us -> 8.91 us
  Pallas kernels: 31.4 us -> 13.3 us
  starting transfers between devices: 19.3 us -> 14.5 us
  local copies, waits for them, and re-layouts: 3.3 us -> 1.62 us
    all_to_all x0 -> x1, blocking collectives: none -> 26.7 us  [per_device(): got = lax.all_to_all(routed, ('row', 'col'), 0, 0, tiled=True)]
    pallas_call x1, Pallas kernels: 26.7 us -> 8.2 us  [per_device(): pl.pallas_call(join_kernel, out_shape=jax.ShapeDtypeStruct((FOLD, LANES),...]
    all_to_all x1, waiting for transfers between devices: 16.1 us -> 5.02 us  [per_device(): spread = lax.all_to_all(sent, ('row', 'col'), 0, 0, tiled=True)]
    all_to_all x1 -> x0, waiting for transfers between devices: 7.43 us -> none  [per_device(): got = lax.all_to_all(routed, ('row', 'col'), 0, 0, tiled=True)]
    all_to_all x1 -> x0, starting transfers between devices: 4.89 us -> none  [per_device(): got = lax.all_to_all(routed, ('row', 'col'), 0, 0, tiled=True)]
    ppermute x1, waiting for transfers between devices: 8.58 us -> 3.89 us  [per_device(): lax.ppermute(heads, ('row', 'col'), [(i + 1, i) for i in range(DEVS - 1)])]
    unnamed x12 -> x8, local copies, waits for them, and re-layouts: 1.75 us -> 0.01 us
    pallas_call x1, Pallas kernels: 1.98 us -> 3.24 us  [per_device(): pl.pallas_call(scatter_kernel, out_shape=jax.ShapeDtypeStruct((DEVS, SLOT...]
  transfers between devices with their start and end apart: 3 -> 2, of which waited for: 3 -> 2; matrix products, arithmetic and copies ran while one was open for 2% -> 5% of each run, Pallas kernels for 0% -> 0%
where the time goes in v2:
time: 68.5 us; the launch traced here: 68.3 us
  blocking collectives  26.7 us (39%)
  starting transfers between devices  14.5 us (21%)
  Pallas kernels  13.3 us (19%)
  waiting for transfers between devices  8.91 us (13%)
  other arithmetic  2.53 us (4%)
  local copies, waits for them, and re-layouts  1.62 us (2%)
  between operations  0.8 us (1%)
    all_to_all x1, blocking collectives, per_device(): got = lax.all_to_all(routed, ('row', 'col'), 0, 0, tiled=True)  26.7 us
    all_to_all x1, starting transfers between devices, per_device(): spread = lax.all_to_all(sent, ('row', 'col'), 0, 0, tiled=True)  11.5 us
    pallas_call x1, Pallas kernels, per_device(): pl.pallas_call(join_kernel, out_shape=jax.ShapeDtypeStruct((FOLD, LANES),...  8.2 us
    all_to_all x1, waiting for transfers between devices, per_device(): spread = lax.all_to_all(sent, ('row', 'col'), 0, 0, tiled=True)  5.02 us
    ppermute x1, waiting for transfers between devices, per_device(): lax.ppermute(heads, ('row', 'col'), [(i + 1, i) for i in range(DEVS - 1)])  3.89 us
    pallas_call x1, Pallas kernels, per_device(): pl.pallas_call(scatter_kernel, out_shape=jax.ShapeDtypeStruct((DEVS, SLOT...  3.24 us
    ppermute x1, starting transfers between devices, per_device(): lax.ppermute(heads, ('row', 'col'), [(i + 1, i) for i in range(DEVS - 1)])  2.98 us
    pallas_call x1, Pallas kernels, per_device(): pl.pallas_call(route_kernel, out_shape=jax.ShapeDtypeStruct((DEVS, SLOT2,...  1.56 us
  transfers between devices with their start and end apart: 2, of which 2 were waited for; matrix products, arithmetic and copies ran while one was open for 5% of the time, Pallas kernels for 0%

profile of v2, /device:TPU:1, one launch (start us, length us, event | category | flops | bytes accessed | tf_op | source)
XLA Modules:
  0.0 68.3 jit_solution(4735040263338135211)
XLA Ops:
  0.0 3.2 %shard_map.46 = bf16[128,24,128]{2,1,0:T(8,128)(2,1)} custom-call(bf16[2048,128]{1,0:T(8,128)(2,1)} %own_ref, s32[16,128]{1,0:T(8,128)} %bitcast.10), custom_call_target="tpu_custom_call" | custom-call | tf_op jit(solution)/shard_map/pallas_call | solution.py:260
  3.3 11.5 %all-to-all-start = ((bf16[128,24,128]{2,1,0:T(8,128)(2,1)}), bf16[128,24,128]{2,1,0:T(8,128)(2,1)S(1)}, u32[]{:S(2)}, u32[]{:S(2)}) async-start(bf16[128,24,128]{2,1,0:T(8,128)(2,1)} %shard_map.46), calls=%async_computation | async-start | bytes 1572864 | tf_op jit(solution)/shard_map/all_to_all | solution.py:269
  14.7 0.0 copy-done.2
  14.8 0.0 slice-done
  14.8 3.0 %collective-permute-start = (bf16[72,128]{1,0:T(8,128)(2,1)S(1)}, bf16[72,128]{1,0:T(8,128)(2,1)S(1)}, u32[]{:S(2)}, u32[]{:S(2)}) collective-permute-start(bf16[72,128]{1,0:T(8,128)(2,1)S(1)} %pad_maximum_fusion), channel_id=1, source_target_pairs={{1,0},{2,1},{3,2},{4,3},{5,4},{6,5},{7,6},{8,7},{9,8},{10,9},{11,1... | collective-permute-start | bytes 55304 | tf_op jit(solution)/shard_map/ppermute | solution.py:272
  17.8 0.0 copy-done
  17.8 0.3 multiply_reduce_fusion
  18.2 0.0 copy-done.3
  18.2 0.2 fusion.255
  18.4 0.0 copy-done.1
  18.4 0.6 gather_fusion
  19.0 0.1 pad_add_fusion.1.info_ref
  19.1 0.6 dynamic_slice.7
  20.4 3.9 %collective-permute-done.head_ref = bf16[72,128]{1,0:T(8,128)(2,1)S(1)} collective-permute-done((bf16[72,128]{1,0:T(8,128)(2,1)S(1)}, bf16[72,128]{1,0:T(8,128)(2,1)S(1)}, u32[]{:S(2)}, u32[]{:S(2)}) %collective-permute-start) | collective-permute-done | bytes 18464 | tf_op jit(solution)/shard_map/ppermute | solution.py:272
  24.3 0.3 shard_map.47.right_ref.right
  24.6 0.1 multiply_reduce_fusion.1
  24.7 1.1 %fusion.3.norm_ref = f32[2048]{0:T(1024)S(1)} fusion(f32[2048]{0:T(1024)S(1)} %multiply_reduce_fusion, f32[64]{0:T(128)S(1)} %multiply_reduce_fusion.1, f32[64]{0:T(128)S(1)} %fusion.256, f32[2048]{0:T(1024)S(1)} %convert_element_type.20, s32[]{:T(128)} %bitcast, pred[]{:T(512)S(6)} %and.11), kind=kLoop, calls=%fused_computation.255 | loop fusion | flops 526336 | bytes 25093 | tf_op jit(solution)/shard_map/jit(_where)/select_n | solution.py:297
  25.8 5.0 %all-to-all-done.got_ref = bf16[128,24,128]{2,1,0:T(8,128)(2,1)S(1)} async-done(((bf16[128,24,128]{2,1,0:T(8,128)(2,1)}), bf16[128,24,128]{2,1,0:T(8,128)(2,1)S(1)}, u32[]{:S(2)}, u32[]{:S(2)}) %all-to-all-start) | async-done | bytes 786464 | tf_op jit(solution)/shard_map/all_to_all | solution.py:269
  30.9 1.6 %shard_map.48 = bf16[128,40,128]{2,1,0:T(8,128)(2,1)S(1)} custom-call(s32[4,128]{1,0:T(4,128)S(1)} %pad_add_fusion.pick_ref, bf16[128,24,128]{2,1,0:T(8,128)(2,1)S(1)} %all-to-all-done.got_ref, s32[7]{0:T(128)S(1)} %pad_add_fusion.1.info_ref, bf16[2176,256]{1,0:T(8,128)(2,1)S(1)} %shard_map.47.right_ref.right, f32[2048]{0:T(1024)S(1)} %fusion.3.norm_ref), custom_call_target="tpu_custom_call" | custom-call | tf_op jit(solution)/shard_map/pallas_call | solution.py:307
  32.4 26.7 %all_to_all.10.got_ref = bf16[128,40,128]{2,1,0:T(8,128)(2,1)S(1)} all-to-all(bf16[128,40,128]{2,1,0:T(8,128)(2,1)S(1)} %shard_map.48), channel_id=1, replica_groups=mesh['row'=8,'col'=16] {'row','col'}, dimensions={0} | all-to-all | bytes 2621440 | tf_op jit(solution)/shard_map/all_to_all | solution.py:314
  59.1 8.2 %shard_map.49 = f32[17,128]{1,0:T(8,128)S(1)} custom-call(s32[7]{0:T(128)S(1)} %pad_add_fusion.1.info_ref, bf16[128,40,128]{2,1,0:T(8,128)(2,1)S(1)} %all_to_all.10.got_ref, bf16[2176,256]{1,0:T(8,128)(2,1)S(1)} %shard_map.47.right_ref.right), custom_call_target="tpu_custom_call" | custom-call | tf_op jit(solution)/shard_map/pallas_call | solution.py:315
  67.3 0.1 copy.5
  67.4 0.2 reshape.11
  67.6 0.7 fusion.252
  (14 shorter events, 0.1 us)
Async XLA Ops:
  0.0 14.7 %copy-start.2 = (s32[2048]{0:T(1024)S(1)}, s32[2048]{0:T(1024)}, u32[]{:S(2)}) copy-start(s32[2048]{0:T(1024)} %param.5) | copy-start | bytes 24580
  0.0 14.8 %slice-start = ((bf16[2048,128]{1,0:T(8,128)(2,1)}), bf16[64,128]{1,0:T(8,128)(2,1)S(1)}, s32[]{:S(2)}) async-start(bf16[2048,128]{1,0:T(8,128)(2,1)} %own_ref), calls=%async_computation.2 | async-start | bytes 32768 | tf_op jit(solution)/shard_map/slice | solution.py:271
  0.0 17.8 %copy-start = (bf16[2048,128]{1,0:T(8,128)(2,1)S(1)}, bf16[2048,128]{1,0:T(8,128)(2,1)}, u32[]{:S(2)}) copy-start(bf16[2048,128]{1,0:T(8,128)(2,1)} %own_ref) | copy-start | bytes 1572868
  3.2 14.9 %copy-start.3 = (s32[2,128]{1,0:T(2,128)S(1)}, s32[2,128]{1,0:T(2,128)}, u32[]{:S(2)}) copy-start(s32[2,128]{1,0:T(2,128)} %param.7) | copy-start | bytes 3076
  3.2 15.1 %copy-start.1 = (s32[128]{0:T(128)S(1)}, s32[128]{0:T(128)}, u32[]{:S(2)}) copy-start(s32[128]{0:T(128)} %param.6) | copy-start | bytes 1540
  3.3 27.6 %all-to-all-start = ((bf16[128,24,128]{2,1,0:T(8,128)(2,1)}), bf16[128,24,128]{2,1,0:T(8,128)(2,1)S(1)}, u32[]{:S(2)}, u32[]{:S(2)}) async-start(bf16[128,24,128]{2,1,0:T(8,128)(2,1)} %shard_map.46), calls=%async_computation | async-start | bytes 1572864 | tf_op jit(solution)/shard_map/all_to_all | solution.py:269
  14.8 9.5 %collective-permute-start = (bf16[72,128]{1,0:T(8,128)(2,1)S(1)}, bf16[72,128]{1,0:T(8,128)(2,1)S(1)}, u32[]{:S(2)}, u32[]{:S(2)}) collective-permute-start(bf16[72,128]{1,0:T(8,128)(2,1)S(1)} %pad_maximum_fusion), channel_id=1, source_target_pairs={{1,0},{2,1},{3,2},{4,3},{5,4},{6,5},{7,6},{8,7},{9,8},{10,9},{11,1... | collective-permute-start | bytes 55304 | tf_op jit(solution)/shard_map/ppermute | solution.py:272

commit v3 on v2

--- a/solution.py
+++ b/solution.py
@@ -20,8 +20,7 @@
 CHUNK = 16
 SLOT = 24
 SLOT2 = 40
-EARLY = True
-BLOCK = 512
+BLOCK = 256
 DEAD = float(2**24)
 F32 = jnp.float32
 BF16 = jnp.bfloat16
@@ -57,7 +56,7 @@
         out_ref[k, CHUNK:SLOT, :] = rest.astype(BF16)
         return 0
 
-    lax.fori_loop(0, DEVS, one, 0, unroll=4)
+    lax.fori_loop(0, DEVS, one, 0, unroll=16)
 
 
 def route_kernel(pick_ref, got_ref, info_ref, right_ref, norm_ref, out_ref):
@@ -213,7 +212,7 @@
     for b in range(blocks):
         if b + 1 < blocks:
             dot(b + 1, prods[(b + 1) % 2])
-        goal = min((b + 1) * steps - (SPAN - 1) + (steps if EARLY else 0), count)
+        goal = min((b + 1) * steps - (SPAN - 1), count)
         if goal > made:
             energy = norms(energy, made, goal)
             made = goal

time: 68.5 us -> 68.1 us (level)
  no operation moved by 1% of the time
where the time goes in v3:
time: 68.1 us; the launch traced here: 67.9 us
  blocking collectives  26.7 us (39%)
  starting transfers between devices  14.5 us (21%)
  Pallas kernels  12.9 us (19%)
  waiting for transfers between devices  8.91 us (13%)
  other arithmetic  2.53 us (4%)
  local copies, waits for them, and re-layouts  1.62 us (2%)
  between operations  0.8 us (1%)
    all_to_all x1, blocking collectives, per_device(): got = lax.all_to_all(routed, ('row', 'col'), 0, 0, tiled=True)  26.7 us
    all_to_all x1, starting transfers between devices, per_device(): spread = lax.all_to_all(sent, ('row', 'col'), 0, 0, tiled=True)  11.5 us
    pallas_call x1, Pallas kernels, per_device(): pl.pallas_call(join_kernel, out_shape=jax.ShapeDtypeStruct((FOLD, LANES),...  7.98 us
    all_to_all x1, waiting for transfers between devices, per_device(): spread = lax.all_to_all(sent, ('row', 'col'), 0, 0, tiled=True)  5.02 us
    ppermute x1, waiting for transfers between devices, per_device(): lax.ppermute(heads, ('row', 'col'), [(i + 1, i) for i in range(DEVS - 1)])  3.89 us
    pallas_call x1, Pallas kernels, per_device(): pl.pallas_call(scatter_kernel, out_shape=jax.ShapeDtypeStruct((DEVS, SLOT...  3.03 us
    ppermute x1, starting transfers between devices, per_device(): lax.ppermute(heads, ('row', 'col'), [(i + 1, i) for i in range(DEVS - 1)])  2.98 us
    pallas_call x1, Pallas kernels, per_device(): pl.pallas_call(route_kernel, out_shape=jax.ShapeDtypeStruct((DEVS, SLOT2,...  1.56 us
  transfers between devices with their start and end apart: 2, of which 2 were waited for; matrix products, arithmetic and copies ran while one was open for 5% of the time, Pallas kernels for 0%

profile of v3, /device:TPU:1, one launch (start us, length us, event | category | flops | bytes accessed | tf_op | source)
XLA Modules:
  0.0 67.9 jit_solution(8491693872520887913)
XLA Ops:
  0.0 3.0 %shard_map.46 = bf16[128,24,128]{2,1,0:T(8,128)(2,1)} custom-call(bf16[2048,128]{1,0:T(8,128)(2,1)} %own_ref, s32[16,128]{1,0:T(8,128)} %bitcast.10), custom_call_target="tpu_custom_call" | custom-call | tf_op jit(solution)/shard_map/pallas_call | solution.py:259
  3.0 11.5 %all-to-all-start = ((bf16[128,24,128]{2,1,0:T(8,128)(2,1)}), bf16[128,24,128]{2,1,0:T(8,128)(2,1)S(1)}, u32[]{:S(2)}, u32[]{:S(2)}) async-start(bf16[128,24,128]{2,1,0:T(8,128)(2,1)} %shard_map.46), calls=%async_computation | async-start | bytes 1572864 | tf_op jit(solution)/shard_map/all_to_all | solution.py:268
  14.5 0.0 copy-done.2
  14.6 0.0 slice-done
  14.6 3.0 %collective-permute-start = (bf16[72,128]{1,0:T(8,128)(2,1)S(1)}, bf16[72,128]{1,0:T(8,128)(2,1)S(1)}, u32[]{:S(2)}, u32[]{:S(2)}) collective-permute-start(bf16[72,128]{1,0:T(8,128)(2,1)S(1)} %pad_maximum_fusion), channel_id=1, source_target_pairs={{1,0},{2,1},{3,2},{4,3},{5,4},{6,5},{7,6},{8,7},{9,8},{10,9},{11,1... | collective-permute-start | bytes 55304 | tf_op jit(solution)/shard_map/ppermute | solution.py:271
  17.6 0.0 copy-done
  17.6 0.3 multiply_reduce_fusion
  17.9 0.0 copy-done.3
  18.0 0.2 fusion.255
  18.2 0.0 copy-done.1
  18.2 0.6 gather_fusion
  18.8 0.1 pad_add_fusion.1.info_ref
  18.9 0.6 dynamic_slice.7
  20.2 3.9 %collective-permute-done.head_ref = bf16[72,128]{1,0:T(8,128)(2,1)S(1)} collective-permute-done((bf16[72,128]{1,0:T(8,128)(2,1)S(1)}, bf16[72,128]{1,0:T(8,128)(2,1)S(1)}, u32[]{:S(2)}, u32[]{:S(2)}) %collective-permute-start) | collective-permute-done | bytes 18464 | tf_op jit(solution)/shard_map/ppermute | solution.py:271
  24.1 0.3 shard_map.47.right_ref.right
  24.4 0.1 multiply_reduce_fusion.1
  24.5 1.1 %fusion.3.norm_ref = f32[2048]{0:T(1024)S(1)} fusion(f32[2048]{0:T(1024)S(1)} %multiply_reduce_fusion, f32[64]{0:T(128)S(1)} %multiply_reduce_fusion.1, f32[64]{0:T(128)S(1)} %fusion.256, f32[2048]{0:T(1024)S(1)} %convert_element_type.20, s32[]{:T(128)} %bitcast, pred[]{:T(512)S(6)} %and.11), kind=kLoop, calls=%fused_computation.255 | loop fusion | flops 526336 | bytes 25093 | tf_op jit(solution)/shard_map/jit(_where)/select_n | solution.py:296
  25.6 5.0 %all-to-all-done.got_ref = bf16[128,24,128]{2,1,0:T(8,128)(2,1)S(1)} async-done(((bf16[128,24,128]{2,1,0:T(8,128)(2,1)}), bf16[128,24,128]{2,1,0:T(8,128)(2,1)S(1)}, u32[]{:S(2)}, u32[]{:S(2)}) %all-to-all-start) | async-done | bytes 786464 | tf_op jit(solution)/shard_map/all_to_all | solution.py:268
  30.7 1.6 %shard_map.48 = bf16[128,40,128]{2,1,0:T(8,128)(2,1)S(1)} custom-call(s32[4,128]{1,0:T(4,128)S(1)} %pad_add_fusion.pick_ref, bf16[128,24,128]{2,1,0:T(8,128)(2,1)S(1)} %all-to-all-done.got_ref, s32[7]{0:T(128)S(1)} %pad_add_fusion.1.info_ref, bf16[2176,256]{1,0:T(8,128)(2,1)S(1)} %shard_map.47.right_ref.right, f32[2048]{0:T(1024)S(1)} %fusion.3.norm_ref), custom_call_target="tpu_custom_call" | custom-call | tf_op jit(solution)/shard_map/pallas_call | solution.py:306
  32.2 26.7 %all_to_all.10.got_ref = bf16[128,40,128]{2,1,0:T(8,128)(2,1)S(1)} all-to-all(bf16[128,40,128]{2,1,0:T(8,128)(2,1)S(1)} %shard_map.48), channel_id=1, replica_groups=mesh['row'=8,'col'=16] {'row','col'}, dimensions={0} | all-to-all | bytes 2621440 | tf_op jit(solution)/shard_map/all_to_all | solution.py:313
  58.9 8.0 %shard_map.49 = f32[17,128]{1,0:T(8,128)S(1)} custom-call(s32[7]{0:T(128)S(1)} %pad_add_fusion.1.info_ref, bf16[128,40,128]{2,1,0:T(8,128)(2,1)S(1)} %all_to_all.10.got_ref, bf16[2176,256]{1,0:T(8,128)(2,1)S(1)} %shard_map.47.right_ref.right), custom_call_target="tpu_custom_call" | custom-call | tf_op jit(solution)/shard_map/pallas_call | solution.py:314
  66.9 0.1 copy.5
  67.0 0.2 reshape.11
  67.2 0.7 fusion.252
  (14 shorter events, 0.1 us)
Async XLA Ops:
  0.0 14.5 %copy-start.2 = (s32[2048]{0:T(1024)S(1)}, s32[2048]{0:T(1024)}, u32[]{:S(2)}) copy-start(s32[2048]{0:T(1024)} %param.5) | copy-start | bytes 24580
  0.0 14.6 %slice-start = ((bf16[2048,128]{1,0:T(8,128)(2,1)}), bf16[64,128]{1,0:T(8,128)(2,1)S(1)}, s32[]{:S(2)}) async-start(bf16[2048,128]{1,0:T(8,128)(2,1)} %own_ref), calls=%async_computation.2 | async-start | bytes 32768 | tf_op jit(solution)/shard_map/slice | solution.py:270
  0.0 17.6 %copy-start = (bf16[2048,128]{1,0:T(8,128)(2,1)S(1)}, bf16[2048,128]{1,0:T(8,128)(2,1)}, u32[]{:S(2)}) copy-start(bf16[2048,128]{1,0:T(8,128)(2,1)} %own_ref) | copy-start | bytes 1572868
  3.0 14.9 %copy-start.3 = (s32[2,128]{1,0:T(2,128)S(1)}, s32[2,128]{1,0:T(2,128)}, u32[]{:S(2)}) copy-start(s32[2,128]{1,0:T(2,128)} %param.7) | copy-start | bytes 3076
  3.0 15.1 %copy-start.1 = (s32[128]{0:T(128)S(1)}, s32[128]{0:T(128)}, u32[]{:S(2)}) copy-start(s32[128]{0:T(128)} %param.6) | copy-start | bytes 1540
  3.0 27.6 %all-to-all-start = ((bf16[128,24,128]{2,1,0:T(8,128)(2,1)}), bf16[128,24,128]{2,1,0:T(8,128)(2,1)S(1)}, u32[]{:S(2)}, u32[]{:S(2)}) async-start(bf16[128,24,128]{2,1,0:T(8,128)(2,1)} %shard_map.46), calls=%async_computation | async-start | bytes 1572864 | tf_op jit(solution)/shard_map/all_to_all | solution.py:268
  14.6 9.5 %collective-permute-start = (bf16[72,128]{1,0:T(8,128)(2,1)S(1)}, bf16[72,128]{1,0:T(8,128)(2,1)S(1)}, u32[]{:S(2)}, u32[]{:S(2)}) collective-permute-start(bf16[72,128]{1,0:T(8,128)(2,1)S(1)} %pad_maximum_fusion), channel_id=1, source_target_pairs={{1,0},{2,1},{3,2},{4,3},{5,4},{6,5},{7,6},{8,7},{9,8},{10,9},{11,1... | collective-permute-start | bytes 55304 | tf_op jit(solution)/shard_map/ppermute | solution.py:271

commit v4 on v3

--- a/solution.py
+++ b/solution.py
@@ -39,7 +39,6 @@
         extra = jnp.where(sub == 0, block, 0.0)
         turned.append(jnp.transpose(jnp.concatenate([block, extra, pad], 0)))
     flags2 = jnp.concatenate(turned, 0)
-    out_ref[:, CHUNK:SLOT, :] = jnp.zeros((DEVS, SUBS, LANES), BF16)
     wide[pl.ds(SEG, 2 * LANES), :] = flags2
 
     def one(k, _):
@@ -90,7 +89,7 @@
     lax.fori_loop(0, DEVS, one, 0, unroll=4)
 
 
-def own_kernel(own_ref, head_ref, out_ref, wide):
+def own_kernel(own_ref, head_ref, out_ref, bands_ref, wide):
     wide[0:SPAN, :] = jnp.zeros((SPAN, LANES), F32)
     wide[pl.ds(SPAN, SEG), :] = own_ref[...].astype(F32)
     wide[pl.ds(SPAN + SEG, SPAN), :] = head_ref[0:SPAN, :].astype(F32)
@@ -101,8 +100,17 @@
         out_ref[j * LANES : (j + 1) * LANES, 0:LANES] = (here * -2.0).astype(BF16)
         out_ref[j * LANES : (j + 1) * LANES, LANES:] = (back * 2.0).astype(BF16)
 
-
-def join_kernel(info_ref, got_ref, right, out_ref, tail, prod0, prod1, extra, gates, bias):
+    row = lax.broadcasted_iota(jnp.int32, (STEP, LANES), 0)
+    column = lax.broadcasted_iota(jnp.int32, (STEP, LANES), 1)
+
+    def band(offset):
+        gap = 2 * column + offset - row
+        return jnp.where((gap >= 1) & (gap < SPAN), 1.0, 0.0).astype(BF16)
+
+    bands_ref[...] = jnp.concatenate([band(0), band(1), band(STEP), band(STEP + 1)], 1)
+
+
+def join_kernel(info_ref, got_ref, right, bands_ref, out_ref, tail, prod0, prod1, extra, gates, bias):
     sub = lax.broadcasted_iota(jnp.int32, (SUBS, LANES), 0)
     lane = lax.broadcasted_iota(jnp.int32, (SUBS, LANES), 1)
     me = info_ref[0]
@@ -131,11 +139,7 @@
     column = lax.broadcasted_iota(jnp.int32, (STEP, LANES), 1)
     place = STEP * column + row
 
-    def band(offset):
-        gap = 2 * column + offset - row
-        return jnp.where((gap >= 1) & (gap < SPAN), 1.0, 0.0).astype(BF16)
-
-    bands = jnp.concatenate([band(0), band(1), band(STEP), band(STEP + 1)], 1)
+    bands = bands_ref[...]
     closed = []
     for part in range(2):
         even = extra[pl.ds(2 * part, DEVS, stride=SUBS), :]
@@ -269,11 +273,14 @@
 
     heads = jnp.concatenate([beats[:SPAN], jnp.broadcast_to(track_marks[None, :LANES].astype(BF16), (SUBS, LANES))], 0)
     head = lax.ppermute(heads, ("row", "col"), [(i + 1, i) for i in range(DEVS - 1)])
-    right = pl.pallas_call(
+    right, bands = pl.pallas_call(
         own_kernel,
-        out_shape=jax.ShapeDtypeStruct((WRAP, 2 * LANES), BF16),
+        out_shape=(
+            jax.ShapeDtypeStruct((WRAP, 2 * LANES), BF16),
+            jax.ShapeDtypeStruct((STEP, 4 * LANES), BF16),
+        ),
         in_specs=[vmem] * 2,
-        out_specs=vmem,
+        out_specs=(vmem, vmem),
         scratch_shapes=[VMEM((SEG + 3 * SPAN, LANES), F32)],
         compiler_params=room(16),
     )(beats, head)
@@ -314,7 +321,7 @@
     best = pl.pallas_call(
         join_kernel,
         out_shape=jax.ShapeDtypeStruct((FOLD, LANES), F32),
-        in_specs=[smem] + [vmem] * 2,
+        in_specs=[smem] + [vmem] * 3,
         out_specs=vmem,
         scratch_shapes=[
             VMEM((SPAN * SUBS, LANES), BF16),
@@ -325,7 +332,7 @@
             VMEM((2 * SEG, LANES), F32),
         ],
         compiler_params=room(36),
-    )(info, got, right)
+    )(info, got, right, bands)
     flat = best.T.reshape(WRAP)[SPAN - 1 : SPAN - 1 + SEG]
     return jnp.minimum((norm + flat) * (1.0 / (SPAN * WIDTH)), CEIL)
 

time: 68.1 us -> 68.2 us (level)
  transfers between devices with their start and end apart: 2 -> 2, of which waited for: 2 -> 2; matrix products, arithmetic and copies ran while one was open for 5% -> 5% of each run, Pallas kernels for 0% -> 1%
where the time goes in v4:
time: 68.2 us; the launch traced here: 67.9 us
  blocking collectives  26.8 us (39%)
  starting transfers between devices  14.5 us (21%)
  Pallas kernels  13 us (19%)
  waiting for transfers between devices  8.79 us (13%)
  other arithmetic  2.53 us (4%)
  local copies, waits for them, and re-layouts  1.62 us (2%)
  between operations  0.8 us (1%)
    all_to_all x1, blocking collectives, per_device(): got = lax.all_to_all(routed, ('row', 'col'), 0, 0, tiled=True)  26.8 us
    all_to_all x1, starting transfers between devices, per_device(): spread = lax.all_to_all(sent, ('row', 'col'), 0, 0, tiled=True)  11.5 us
    pallas_call x1, Pallas kernels, per_device(): pl.pallas_call(join_kernel, out_shape=jax.ShapeDtypeStruct((FOLD, LANES),...  7.96 us
    all_to_all x1, waiting for transfers between devices, per_device(): spread = lax.all_to_all(sent, ('row', 'col'), 0, 0, tiled=True)  4.89 us
    ppermute x1, waiting for transfers between devices, per_device(): lax.ppermute(heads, ('row', 'col'), [(i + 1, i) for i in range(DEVS - 1)])  3.89 us
    pallas_call x1, Pallas kernels, per_device(): pl.pallas_call(scatter_kernel, out_shape=jax.ShapeDtypeStruct((DEVS, SLOT...  3 us
    ppermute x1, starting transfers between devices, per_device(): lax.ppermute(heads, ('row', 'col'), [(i + 1, i) for i in range(DEVS - 1)])  2.98 us
    pallas_call x1, Pallas kernels, per_device(): pl.pallas_call(route_kernel, out_shape=jax.ShapeDtypeStruct((DEVS, SLOT2,...  1.56 us
  transfers between devices with their start and end apart: 2, of which 2 were waited for; matrix products, arithmetic and copies ran while one was open for 5% of the time, Pallas kernels for 1%

profile of v4, /device:TPU:1, one launch (start us, length us, event | category | flops | bytes accessed | tf_op | source)
XLA Modules:
  0.0 67.9 jit_solution(4520536600176662569)
XLA Ops:
  0.0 3.0 %shard_map.46 = bf16[128,24,128]{2,1,0:T(8,128)(2,1)} custom-call(bf16[2048,128]{1,0:T(8,128)(2,1)} %own_ref, s32[16,128]{1,0:T(8,128)} %bitcast.10), custom_call_target="tpu_custom_call" | custom-call | tf_op jit(solution)/shard_map/pallas_call | solution.py:263
  3.0 11.5 %all-to-all-start = ((bf16[128,24,128]{2,1,0:T(8,128)(2,1)}), bf16[128,24,128]{2,1,0:T(8,128)(2,1)S(1)}, u32[]{:S(2)}, u32[]{:S(2)}) async-start(bf16[128,24,128]{2,1,0:T(8,128)(2,1)} %shard_map.46), calls=%async_computation | async-start | bytes 1572864 | tf_op jit(solution)/shard_map/all_to_all | solution.py:272
  14.5 0.0 copy-done.2
  14.5 0.0 slice-done
  14.6 3.0 %collective-permute-start = (bf16[72,128]{1,0:T(8,128)(2,1)S(1)}, bf16[72,128]{1,0:T(8,128)(2,1)S(1)}, u32[]{:S(2)}, u32[]{:S(2)}) collective-permute-start(bf16[72,128]{1,0:T(8,128)(2,1)S(1)} %pad_maximum_fusion), channel_id=1, source_target_pairs={{1,0},{2,1},{3,2},{4,3},{5,4},{6,5},{7,6},{8,7},{9,8},{10,9},{11,1... | collective-permute-start | bytes 55304 | tf_op jit(solution)/shard_map/ppermute | solution.py:275
  17.6 0.0 copy-done
  17.6 0.3 multiply_reduce_fusion
  17.9 0.0 copy-done.3
  17.9 0.2 fusion.255
  18.1 0.0 copy-done.1
  18.2 0.6 gather_fusion
  18.8 0.1 pad_add_fusion.1.info_ref
  18.9 0.6 dynamic_slice.7
  20.2 3.9 %collective-permute-done.head_ref = bf16[72,128]{1,0:T(8,128)(2,1)S(1)} collective-permute-done((bf16[72,128]{1,0:T(8,128)(2,1)S(1)}, bf16[72,128]{1,0:T(8,128)(2,1)S(1)}, u32[]{:S(2)}, u32[]{:S(2)}) %collective-permute-start) | collective-permute-done | bytes 18464 | tf_op jit(solution)/shard_map/ppermute | solution.py:275
  24.1 0.4 shard_map.47
  24.5 0.1 multiply_reduce_fusion.1
  24.6 1.1 %fusion.3.norm_ref = f32[2048]{0:T(1024)S(1)} fusion(f32[2048]{0:T(1024)S(1)} %multiply_reduce_fusion, f32[64]{0:T(128)S(1)} %multiply_reduce_fusion.1, f32[64]{0:T(128)S(1)} %fusion.256, f32[2048]{0:T(1024)S(1)} %convert_element_type.20, s32[]{:T(128)} %bitcast, pred[]{:T(512)S(6)} %and.11), kind=kLoop, calls=%fused_computation.255 | loop fusion | flops 526336 | bytes 25093 | tf_op jit(solution)/shard_map/jit(_where)/select_n | solution.py:303
  25.7 4.9 %all-to-all-done.got_ref = bf16[128,24,128]{2,1,0:T(8,128)(2,1)S(1)} async-done(((bf16[128,24,128]{2,1,0:T(8,128)(2,1)}), bf16[128,24,128]{2,1,0:T(8,128)(2,1)S(1)}, u32[]{:S(2)}, u32[]{:S(2)}) %all-to-all-start) | async-done | bytes 786464 | tf_op jit(solution)/shard_map/all_to_all | solution.py:272
  30.6 1.6 %shard_map.48 = bf16[128,40,128]{2,1,0:T(8,128)(2,1)S(1)} custom-call(s32[4,128]{1,0:T(4,128)S(1)} %pad_add_fusion.pick_ref, bf16[128,24,128]{2,1,0:T(8,128)(2,1)S(1)} %all-to-all-done.got_ref, s32[7]{0:T(128)S(1)} %pad_add_fusion.1.info_ref, bf16[2176,256]{1,0:T(8,128)(2,1)S(1)} %get-tuple-element.13.right_ref.right, f32[2048]{0:T(1024)S(1)} %fusion.3.norm_ref), custom_call_target="tpu_custom_call" | custom-call | tf_op jit(solution)/shard_map/pallas_call | solution.py:313
  32.2 26.8 %all_to_all.10.got_ref = bf16[128,40,128]{2,1,0:T(8,128)(2,1)S(1)} all-to-all(bf16[128,40,128]{2,1,0:T(8,128)(2,1)S(1)} %shard_map.48), channel_id=1, replica_groups=mesh['row'=8,'col'=16] {'row','col'}, dimensions={0} | all-to-all | bytes 2621440 | tf_op jit(solution)/shard_map/all_to_all | solution.py:320
  59.0 8.0 %shard_map.49 = f32[17,128]{1,0:T(8,128)S(1)} custom-call(s32[7]{0:T(128)S(1)} %pad_add_fusion.1.info_ref, bf16[128,40,128]{2,1,0:T(8,128)(2,1)S(1)} %all_to_all.10.got_ref, bf16[2176,256]{1,0:T(8,128)(2,1)S(1)} %get-tuple-element.13.right_ref.right, bf16[256,512]{1,0:T(8,128)(2,1)S(1)} %get-tuple-element.14.bands_ref), custom_call_target="tpu_custom_call" | custom-call | tf_op jit(solution)/shard_map/pallas_call | solution.py:321
  66.9 0.1 copy.5
  67.1 0.2 reshape.11
  67.3 0.7 fusion.252
  (14 shorter events, 0.1 us)
Async XLA Ops:
  0.0 14.5 %copy-start.2 = (s32[2048]{0:T(1024)S(1)}, s32[2048]{0:T(1024)}, u32[]{:S(2)}) copy-start(s32[2048]{0:T(1024)} %param.5) | copy-start | bytes 24580
  0.0 14.5 %slice-start = ((bf16[2048,128]{1,0:T(8,128)(2,1)}), bf16[64,128]{1,0:T(8,128)(2,1)S(1)}, s32[]{:S(2)}) async-start(bf16[2048,128]{1,0:T(8,128)(2,1)} %own_ref), calls=%async_computation.2 | async-start | bytes 32768 | tf_op jit(solution)/shard_map/slice | solution.py:274
  0.0 17.5 %copy-start = (bf16[2048,128]{1,0:T(8,128)(2,1)S(1)}, bf16[2048,128]{1,0:T(8,128)(2,1)}, u32[]{:S(2)}) copy-start(bf16[2048,128]{1,0:T(8,128)(2,1)} %own_ref) | copy-start | bytes 1572868
  3.0 14.9 %copy-start.3 = (s32[2,128]{1,0:T(2,128)S(1)}, s32[2,128]{1,0:T(2,128)}, u32[]{:S(2)}) copy-start(s32[2,128]{1,0:T(2,128)} %param.7) | copy-start | bytes 3076
  3.0 15.1 %copy-start.1 = (s32[128]{0:T(128)S(1)}, s32[128]{0:T(128)}, u32[]{:S(2)}) copy-start(s32[128]{0:T(128)} %param.6) | copy-start | bytes 1540
  3.0 27.6 %all-to-all-start = ((bf16[128,24,128]{2,1,0:T(8,128)(2,1)}), bf16[128,24,128]{2,1,0:T(8,128)(2,1)S(1)}, u32[]{:S(2)}, u32[]{:S(2)}) async-start(bf16[128,24,128]{2,1,0:T(8,128)(2,1)} %shard_map.46), calls=%async_computation | async-start | bytes 1572864 | tf_op jit(solution)/shard_map/all_to_all | solution.py:272
  14.6 9.5 %collective-permute-start = (bf16[72,128]{1,0:T(8,128)(2,1)S(1)}, bf16[72,128]{1,0:T(8,128)(2,1)S(1)}, u32[]{:S(2)}, u32[]{:S(2)}) collective-permute-start(bf16[72,128]{1,0:T(8,128)(2,1)S(1)} %pad_maximum_fusion), channel_id=1, source_target_pairs={{1,0},{2,1},{3,2},{4,3},{5,4},{6,5},{7,6},{8,7},{9,8},{10,9},{11,1... | collective-permute-start | bytes 55304 | tf_op jit(solution)/shard_map/ppermute | solution.py:275
